TPU v7x, 128 devices: a whole 4x4x4 slice. The times are simulated.
128 devices in a mesh: frame: 8 (over y, core), head: 8 (over x_hi, z), fsdp: 2 (over x_lo).
Axes of the slice: x: 4 (x_hi: 2, x_lo: 2; x = x_hi * 2 + x_lo), y: 4, z: 4, core: 2. Of those that a mesh axis runs over, the one named last changes fastest.
Arguments:
- queries: bfloat16 [2, 16, 256, 5120], P('fsdp', 'frame', 'head'), may hold values from -6 to 6
- key_rows: bfloat16 [2, 16, 256, 5120], P('fsdp', 'frame', 'head'), may hold values from -6 to 6
- value_rows: bfloat16 [2, 16, 256, 5120], P('fsdp', 'frame', 'head'), may hold values from -6 to 6
- saved_out: bfloat16 [2, 16, 256, 5120], P('fsdp', 'frame', 'head'), may hold values from -6 to 6
- cotangent: bfloat16 [2, 16, 256, 5120], P('fsdp', 'frame', 'head'), may hold values from -192 to 192
- out_weight: bfloat16 [5120, 5120], P('head'), may hold values from -0.078125 to 0.078125
- gate_table: float32 [64, 5120], replicated, may hold values from 0.25 to 2.5
- levels: int32 [16], P('frame'), may hold values from 0 to 63, as said below
- reach_flags: int32 [16, 2], replicated, may hold values from 0 to 1
Outputs:
- d_queries: bfloat16 [2, 16, 256, 5120], P('fsdp', 'frame', None, 'head')
- d_keys: bfloat16 [2, 16, 256, 5120], P('fsdp', 'frame', None, 'head')
- d_values: bfloat16 [2, 16, 256, 5120], P('fsdp', 'frame', None, 'head')
- d_weight: float32 [5120, 5120], P('head', ('frame', 'fsdp'))
Inputs may be any that keep to these rules, and one draw needn't show every extreme that they name: `levels`: each frame's level is at least the level of the frame before it; the first frame has level 0 and the last frame level 63.
All inputs are finite; a program needn't handle non-finite values.
Results may differ from a plain program's by a relative error of at most 0.017.
Values may be sent and summed in bfloat16 or wider, within the bound.
A program may use at most 128 MiB of HBM per device.

v0:
```python
import functools

import jax
import jax.numpy as jnp
from jax import lax
from jax.experimental import pallas as pl
from jax.experimental.pallas import tpu as pltpu
from jax.sharding import PartitionSpec as P

HD = 128
LEVELS = 64
TOKF = 256
NEG = -1e30
LOG2E = 1.4426950408889634
MESH = pl.DeviceIdType.MESH

NT = (((1,), (1,)), ((), ()))
NN = (((1,), (0,)), ((), ()))


def dot(a, b, dims):
    return lax.dot_general(a, b, dims, preferred_element_type=jnp.float32)


def kernel(
    tokens_all, flags,
    q_hbm, k_hbm, v_hbm, o_hbm, g_hbm, w_hbm,
    dq_hbm, dk_hbm, dv_hbm, dw_hbm,
    w_ref, g_ref, q_ref, o_ref, k_ref, v_ref, ot_ref, dacc, dlow, prob,
    s1_send, s1_recv, gsum, far_send, far_recv, near_send, near_recv, x_send, x_recv, dw_ref,
    own_k, own_v, h_send, h_recv, dq_ref, dk_ref, dv_ref,
    loc_sem, ex_send, ex_recv, ag_send, ag_recv, halo_ssem, halo_rsem,
    s1_ssem, s1_rsem, far_ssem, far_rsem, near_ssem, near_rsem, x_ssem, x_rsem, hg_ssem, hg_rsem, out_sem,
):
    f, h, s = lax.axis_index("frame"), lax.axis_index("head"), lax.axis_index("fsdp")
    nf = 8
    nh = 8
    y, c = f // 2, f % 2
    right, left = (f + 1) % nf, (f + 7) % nf
    up, down = (f + 2) % nf, (f + 6) % nf
    pair = 2 * y + 1 - c
    rows = 32
    wid = 640
    inv_root = HD ** (-0.5)

    def col(j):
        return pl.ds(pl.multiple_of(j * wid, 128), wid)

    my_rows = pl.ds(pl.multiple_of(h * rows, 32), rows)

    def chunk_of(t2):
        t = t2 // 2
        step = jnp.where(t == 0, 2, jnp.where(t == 1, 1, jnp.where(t == 2, 3, 0)))
        yt = (y + step) % 4
        return 2 * yt + jnp.where(t2 % 2 == 0, 1 - c, c)

    w_copy = pltpu.make_async_copy(w_hbm, w_ref, loc_sem.at[0])
    locals_ = [
        pltpu.make_async_copy(k_hbm.at[:, :, col(h)], k_ref.at[pl.ds(1, 2), my_rows, :], loc_sem.at[1]),
        pltpu.make_async_copy(v_hbm.at[:, :, col(h)], v_ref.at[pl.ds(1, 2), my_rows, :], loc_sem.at[2]),
        pltpu.make_async_copy(q_hbm.at[:, :, col(h)], q_ref.at[:, my_rows, :], loc_sem.at[3]),
        pltpu.make_async_copy(o_hbm.at[:, :, col(h)], o_ref.at[:, my_rows, :], loc_sem.at[4]),
        pltpu.make_async_copy(g_hbm, g_ref.at[:, my_rows, :], loc_sem.at[5]),
    ]

    barrier = pltpu.get_barrier_semaphore()
    for p in range(1, nh):
        pl.semaphore_signal(barrier, inc=1, device_id={"head": (h + p) % nh}, device_id_type=MESH)
    for other in (right, left, up, down):
        pl.semaphore_signal(barrier, inc=1, device_id={"frame": other}, device_id_type=MESH)
    pl.semaphore_signal(barrier, inc=1, device_id={"fsdp": 1 - s}, device_id_type=MESH)
    for copy in locals_:
        copy.start()
    w_copy.start()
    pl.semaphore_wait(barrier, nh - 1 + 5)

    def exchange(i, p):
        d = (h + p) % nh
        src, dst = [
            (k_hbm, k_ref.at[pl.ds(1, 2), my_rows, :]),
            (v_hbm, v_ref.at[pl.ds(1, 2), my_rows, :]),
            (q_hbm, q_ref.at[:, my_rows, :]),
            (o_hbm, o_ref.at[:, my_rows, :]),
        ][i]
        return pltpu.make_async_remote_copy(
            src_ref=src.at[:, :, col(d)], dst_ref=dst, send_sem=ex_send.at[i, p], recv_sem=ex_recv.at[i, p],
            device_id={"head": d}, device_id_type=MESH,
        )

    def gather(t2, p):
        d = (h + p) % nh
        cols = col(chunk_of(t2))
        return pltpu.make_async_remote_copy(
            src_ref=g_hbm.at[:, :, cols], dst_ref=g_ref.at[:, my_rows, cols],
            send_sem=ag_send.at[t2, p], recv_sem=ag_recv.at[t2, p],
            device_id={"head": d}, device_id_type=MESH,
        )

    order = (4, 2, 6, 1, 7, 3, 5)
    for i in range(4):
        for p in order:
            exchange(i, p).start()

    @pl.loop(0, 8)
    def _(t2):
        for p in order:
            gather(t2, p).start()

    def halo(i, which):
        ref = (k_ref, v_ref)[i]
        return pltpu.make_async_remote_copy(
            src_ref=ref.at[2 if which == 0 else 1], dst_ref=ref.at[0 if which == 0 else 3],
            send_sem=halo_ssem.at[i, which], recv_sem=halo_rsem.at[i, which],
            device_id={"frame": right if which == 0 else left}, device_id_type=MESH,
        )

    for i in range(2):
        locals_[i].wait()
        for p in range(1, nh):
            exchange(i, p).wait_recv()
        halo(i, 0).start()
        halo(i, 1).start()
    locals_[2].wait()
    for p in range(1, nh):
        exchange(2, p).wait_recv()
    halo(0, 0).wait_recv()
    halo(0, 1).wait_recv()

    def bias_of(fr, column, offset):
        target = fr + offset
        inside = (target >= 0) & (target < 2 * nf)
        chosen = flags[fr, column] == 1
        first = jnp.where(inside, 0.0, NEG).astype(jnp.float32)
        second = jnp.where(inside & chosen, 0.0, NEG).astype(jnp.float32)
        return first, second

    @pl.loop(0, 5)
    def _(hh):
        hs = pl.ds(pl.multiple_of(hh * HD, 128), HD)
        for lf in range(2):
            q = q_ref[lf, :, hs]
            parts = []
            for w in range(3):
                sc = dot(k_ref[lf + w, :, hs], q, NT) * (inv_root * LOG2E)
                if w == 1:
                    parts.append(sc)
                else:
                    first, second = bias_of(2 * f + lf, 0 if w == 0 else 1, w - 1)
                    parts.append(jnp.concatenate([sc[:128] + first, sc[128:] + second], axis=0))
            m = functools.reduce(jnp.maximum, [jnp.max(z, axis=0, keepdims=True) for z in parts])
            parts = [jnp.exp2(z - m) for z in parts]
            total = functools.reduce(jnp.add, [jnp.sum(z, axis=0, keepdims=True) for z in parts])
            inv = 1.0 / total
            for w in range(3):
                prob[2 * hh + lf, pl.ds(w * TOKF, TOKF), :] = parts[w] * inv

    locals_[3].wait()
    for p in range(1, nh):
        exchange(3, p).wait_recv()
    for lf in range(2):
        ot_ref[:, pl.ds(lf * TOKF, TOKF)] = o_ref[lf].astype(jnp.float32).T.astype(jnp.bfloat16)
    locals_[4].wait()
    w_copy.wait()
    dacc[...] = jnp.zeros_like(dacc)

    def s1(t):
        return pltpu.make_async_remote_copy(
            src_ref=s1_send.at[t], dst_ref=s1_recv.at[t], send_sem=s1_ssem.at[t], recv_sem=s1_rsem.at[t],
            device_id={"frame": pair}, device_id_type=MESH,
        )

    def far(i):
        return pltpu.make_async_remote_copy(
            src_ref=far_send.at[i], dst_ref=far_recv.at[i], send_sem=far_ssem.at[i], recv_sem=far_rsem.at[i],
            device_id={"frame": up if i == 0 else down}, device_id_type=MESH,
        )

    def near(i):
        return pltpu.make_async_remote_copy(
            src_ref=near_send.at[i], dst_ref=near_recv.at[i], send_sem=near_ssem.at[i], recv_sem=near_rsem.at[i],
            device_id={"frame": up if i == 0 else down}, device_id_type=MESH,
        )

    def one_chunk(t2):
        for p in range(1, nh):
            gather(t2, p).wait_recv()
        cols = col(chunk_of(t2))
        rhs = g_ref[:, :, cols].reshape(2 * TOKF, wid)
        dacc[...] += dot(rhs, w_ref[:, cols], NT)
        return dot(ot_ref[...], rhs, NN) * (1.0 / tokens_all)

    def finish_near(i):
        far(i).wait_recv()
        half = pl.ds(320 * i, 320)
        rest = pl.ds(320 * (1 - i), 320)
        near_send[i, half, :] = (gsum[1 + i, half, :] + far_recv[i].astype(jnp.float32)).astype(jnp.bfloat16)
        near_send[i, rest, :] = gsum[1 + i, rest, :].astype(jnp.bfloat16)
        near(i).start()

    @pl.loop(0, 4)
    def _(t):
        s1_send[t] = one_chunk(2 * t).astype(jnp.bfloat16)
        s1(t).start()

        @pl.when(t == 2)
        def _():
            finish_near(0)

        @pl.when(t == 3)
        def _():
            finish_near(1)

        gsum[t] = one_chunk(2 * t + 1)
        s1(t).wait_recv()
        gsum[t] += s1_recv[t].astype(jnp.float32)

        @pl.when(t == 0)
        def _():
            for i in range(2):
                far_send[i] = gsum[0, pl.ds(320 * i, 320), :].astype(jnp.bfloat16)
                far(i).start()

    for lf in range(2):
        dlow[lf] = dacc[pl.ds(lf * TOKF, TOKF), :].astype(jnp.bfloat16)
    halo(1, 0).wait_recv()
    halo(1, 1).wait_recv()

    x_copy = pltpu.make_async_remote_copy(
        src_ref=x_send, dst_ref=x_recv, send_sem=x_ssem, recv_sem=x_rsem,
        device_id={"fsdp": 1 - s}, device_id_type=MESH,
    )

    def halo_grad(i, hh):
        return pltpu.make_async_remote_copy(
            src_ref=h_send.at[i, hh], dst_ref=h_recv.at[i, hh], send_sem=hg_ssem.at[i, hh], recv_sem=hg_rsem.at[i, hh],
            device_id={"frame": left if i == 0 else right}, device_id_type=MESH,
        )

    @pl.loop(0, 5)
    def _(hh):
        hs = pl.ds(pl.multiple_of(hh * HD, 128), HD)
        gk = []
        gv = []
        for lf in range(2):
            q = q_ref[lf, :, hs]
            d_out = dlow[lf, :, hs]
            delta = jnp.sum(
                (d_out.astype(jnp.float32) * o_ref[lf, :, hs].astype(jnp.float32)).T, axis=0, keepdims=True
            )
            dq_t = jnp.zeros((HD, TOKF), jnp.float32)
            for w in range(3):
                pr = prob[2 * hh + lf, pl.ds(w * TOKF, TOKF), :]
                dp = dot(v_ref[lf + w, :, hs], d_out, NT)
                ds = (pr * (dp - delta)).astype(jnp.bfloat16)
                gv.append(dot(pr.astype(jnp.bfloat16), d_out, NN))
                gk.append(dot(ds, q, NN) * inv_root)
                kt = k_ref[lf + w, :, hs].astype(jnp.float32).T.astype(jnp.bfloat16)
                dq_t = dq_t + dot(kt, ds, NN)
            dq_ref[lf, :, hs] = (dq_t.T * inv_root).astype(jnp.bfloat16)
        h_send[0, hh, 0] = gk[0].astype(jnp.bfloat16)
        h_send[0, hh, 1] = gv[0].astype(jnp.bfloat16)
        h_send[1, hh, 0] = gk[5].astype(jnp.bfloat16)
        h_send[1, hh, 1] = gv[5].astype(jnp.bfloat16)
        halo_grad(0, hh).start()
        halo_grad(1, hh).start()
        own_k[0, :, hs] = gk[1] + gk[3]
        own_k[1, :, hs] = gk[2] + gk[4]
        own_v[0, :, hs] = gv[1] + gv[3]
        own_v[1, :, hs] = gv[2] + gv[4]

    dq_out = pltpu.make_async_copy(dq_ref, dq_hbm, out_sem.at[0])
    dq_out.start()

    near(0).wait_recv()
    near(1).wait_recv()
    gsum[3] += near_recv[0].astype(jnp.float32) + near_recv[1].astype(jnp.float32)
    x_send[...] = gsum[3, :, pl.ds(pl.multiple_of(256 * (1 - s), 128), 384)].astype(jnp.bfloat16)
    x_copy.start()

    @pl.loop(0, 5)
    def _(hh):
        hs = pl.ds(pl.multiple_of(hh * HD, 128), HD)
        halo_grad(0, hh).wait_recv()
        halo_grad(1, hh).wait_recv()
        dk_ref[0, :, hs] = (own_k[0, :, hs] + h_recv[1, hh, 0].astype(jnp.float32)).astype(jnp.bfloat16)
        dk_ref[1, :, hs] = (own_k[1, :, hs] + h_recv[0, hh, 0].astype(jnp.float32)).astype(jnp.bfloat16)
        dv_ref[0, :, hs] = (own_v[0, :, hs] + h_recv[1, hh, 1].astype(jnp.float32)).astype(jnp.bfloat16)
        dv_ref[1, :, hs] = (own_v[1, :, hs] + h_recv[0, hh, 1].astype(jnp.float32)).astype(jnp.bfloat16)

    dk_out = pltpu.make_async_copy(dk_ref, dk_hbm, out_sem.at[1])
    dv_out = pltpu.make_async_copy(dv_ref, dv_hbm, out_sem.at[2])
    dk_out.start()
    dv_out.start()

    x_copy.wait_recv()
    final = gsum[3, :, pl.ds(pl.multiple_of(256 * s, 128), 384)] + x_recv[...].astype(jnp.float32)
    dw_ref[...] = jnp.where(s == 0, final[:, :320], final[:, 64:384])
    dw_out = pltpu.make_async_copy(dw_ref, dw_hbm, out_sem.at[3])
    dw_out.start()

    for i in range(4):
        for p in range(1, nh):
            exchange(i, p).wait_send()

    @pl.loop(0, 8)
    def _(t2):
        for p in range(1, nh):
            gather(t2, p).wait_send()

    for i in range(2):
        for which in range(2):
            halo(i, which).wait_send()
        far(i).wait_send()
        near(i).wait_send()

    @pl.loop(0, 4)
    def _(t):
        s1(t).wait_send()

    @pl.loop(0, 5)
    def _(hh):
        halo_grad(0, hh).wait_send()
        halo_grad(1, hh).wait_send()

    x_copy.wait_send()
    for copy in (dq_out, dk_out, dv_out, dw_out):
        copy.wait()


def per_device(
    queries, key_rows, value_rows, saved_out, cotangent, out_weight, gate_table, levels, reach_flags
):
    frame_dev = queries.shape[1]
    tokens_all = lax.axis_size("fsdp") * frame_dev * lax.axis_size("frame") * TOKF
    choose = (levels[:, None] == jnp.arange(LEVELS, dtype=jnp.int32)[None, :]).astype(jnp.float32)
    frame_gain = jnp.dot(choose, gate_table, precision=lax.Precision.HIGHEST)
    gated = (cotangent.astype(jnp.float32) * frame_gain[None, :, None, :]).astype(jnp.bfloat16)

    bf, f32 = jnp.bfloat16, jnp.float32
    vm = pltpu.VMEM
    dma = pltpu.SemaphoreType.DMA
    hbm = pl.BlockSpec(memory_space=pl.ANY)
    out = jax.ShapeDtypeStruct((2, TOKF, 640), bf)
    dq, dk, dv, dw = pl.pallas_call(
        functools.partial(kernel, tokens_all),
        out_shape=(out, out, out, jax.ShapeDtypeStruct((640, 320), f32)),
        in_specs=[pl.BlockSpec(memory_space=pltpu.SMEM)] + [hbm] * 6,
        out_specs=(hbm,) * 4,
        scratch_shapes=[
            vm((640, 5120), bf),
            vm((2, TOKF, 5120), bf),
            vm((2, TOKF, 640), bf),
            vm((2, TOKF, 640), bf),
            vm((4, TOKF, 640), bf),
            vm((4, TOKF, 640), bf),
            vm((640, 2 * TOKF), bf),
            vm((2 * TOKF, 640), f32),
            vm((2, TOKF, 640), bf),
            vm((10, 3 * TOKF, TOKF), f32),
            vm((4, 640, 640), bf),
            vm((4, 640, 640), bf),
            vm((4, 640, 640), f32),
            vm((2, 320, 640), bf),
            vm((2, 320, 640), bf),
            vm((2, 640, 640), bf),
            vm((2, 640, 640), bf),
            vm((640, 384), bf),
            vm((640, 384), bf),
            vm((640, 320), f32),
            vm((2, TOKF, 640), f32),
            vm((2, TOKF, 640), f32),
            vm((2, 5, 2, TOKF, HD), bf),
            vm((2, 5, 2, TOKF, HD), bf),
            vm((2, TOKF, 640), bf),
            vm((2, TOKF, 640), bf),
            vm((2, TOKF, 640), bf),
            dma((6,)),
            dma((4, 8)), dma((4, 8)),
            dma((8, 8)), dma((8, 8)),
            dma((2, 2)), dma((2, 2)),
            dma((4,)), dma((4,)),
            dma((2,)), dma((2,)),
            dma((2,)), dma((2,)),
            dma(()), dma(()),
            dma((2, 5)), dma((2, 5)),
            dma((4,)),
        ],
        compiler_params=pltpu.CompilerParams(
            collective_id=0, has_side_effects=True, vmem_limit_bytes=67043328
        ),
        name="window_backward",
    )(
        reach_flags, queries[0], key_rows[0], value_rows[0], saved_out[0], gated[0], out_weight
    )
    return (dq[None], dk[None], dv[None], dw)


def solution(mesh):
    in_specs = (
        P("fsdp", "frame", "head", None),
        P("fsdp", "frame", "head", None),
        P("fsdp", "frame", "head", None),
        P("fsdp", "frame", "head", None),
        P("fsdp", "frame", "head", None),
        P("head", None),
        P(),
        P("frame"),
        P(),
    )
    out_specs = (
        P("fsdp", "frame", None, "head"),
        P("fsdp", "frame", None, "head"),
        P("fsdp", "frame", None, "head"),
        P("head", ("frame", "fsdp")),
    )
    return jax.shard_map(
        per_device, mesh=mesh, in_specs=in_specs, out_specs=out_specs, check_vma=False
    )
```

profile of v0, /device:TPU:6, one launch (start us, length us, event | category | flops | bytes accessed | tf_op | source)
XLA Modules:
  0.0 133.6 jit_solution(17040994223523158041)
XLA Ops:
  0.6 0.0 copy-start
  0.6 1.4 %copy.13.flags = s32[16,2]{1,0:T(8,128)} copy(s32[16,2]{0,1:T(2,128)} %param.17) | data formatting | bytes 256 | tf_op args[8]
  2.1 1.9 %fusion.1 = f32[2,5120]{1,0:T(2,128)S(1)} fusion(f32[64,5120]{1,0:T(8,128)} %param.15, s32[2]{0:T(128)} %param.16), kind=kOutput, calls=%fused_computation.2 | convolution fusion | flops 7864448 | bytes 1351688 | tf_op jit(solution)/shard_map/dot_general | solution.py:336
  3.9 0.0 copy-done
  3.9 0.9 fusion.g_hbm
  4.9 123.6 %window_backward.1 = (bf16[2,256,640]{2,1,0:T(8,128)(2,1)}, bf16[2,256,640]{2,1,0:T(8,128)(2,1)}, bf16[2,256,640]{2,1,0:T(8,128)(2,1)}, f32[640,320]{1,0:T(8,128)}) custom-call(s32[16,2]{1,0:T(8,128)} %copy.13.flags, bf16[2,32,5120]{2,1,0:T(8,128)(2,1)} %bitcast.10, bf16[2,32,5120]{2,1,0:T(8,128)(2,1)} %bitcast.11, bf16[2,32,5120]{2,1,0:T(8,128)(2,1)} %bitcast.12, ...), custom_call_target="tpu_custom_call" | custom-call | tf_op jit(solution)/shard_map/window_backward/pallas_call | solution.py:344
  128.5 0.0 copy-start.3
  128.5 0.0 copy-start.2
  128.5 2.5 %copy.14 = f32[640,320]{0,1:T(8,128)} copy(f32[640,320]{1,0:T(8,128)} %get-tuple-element.15) | data formatting | bytes 1638400
  131.1 0.0 copy-done.3
  131.1 0.0 copy-start.1
  131.1 0.8 copy.18
  131.9 0.0 copy-done.2
  131.9 0.8 copy.19
  132.7 0.0 copy-done.1
  132.7 0.8 copy.20
Async XLA Ops:
  0.6 3.3 %copy-start = (bf16[1,2,32,5120]{3,2,1,0:T(8,128)(2,1)S(1)}, bf16[1,2,32,5120]{3,2,1,0:T(8,128)(2,1)}, u32[]{:S(2)}) copy-start(bf16[1,2,32,5120]{3,2,1,0:T(8,128)(2,1)} %param.13) | copy-start | bytes 1966084
  128.5 2.5 %copy-start.3 = (bf16[2,256,640]{2,1,0:T(8,128)(2,1)S(1)}, bf16[2,256,640]{2,1,0:T(8,128)(2,1)}, u32[]{:S(2)}) copy-start(bf16[2,256,640]{2,1,0:T(8,128)(2,1)} %get-tuple-element.8) | copy-start | bytes 1966084
  128.5 3.4 %copy-start.2 = (bf16[2,256,640]{2,1,0:T(8,128)(2,1)S(1)}, bf16[2,256,640]{2,1,0:T(8,128)(2,1)}, u32[]{:S(2)}) copy-start(bf16[2,256,640]{2,1,0:T(8,128)(2,1)} %get-tuple-element.9) | copy-start | bytes 1966084
  131.1 1.7 %copy-start.1 = (bf16[2,256,640]{2,1,0:T(8,128)(2,1)S(1)}, bf16[2,256,640]{2,1,0:T(8,128)(2,1)}, u32[]{:S(2)}) copy-start(bf16[2,256,640]{2,1,0:T(8,128)(2,1)} %get-tuple-element.10) | copy-start | bytes 1966084
where the time goes:
time: 134 us
  Pallas kernels  124 us (93%)
  local copies, waits for them, and re-layouts  6.45 us (5%)
  matrix products  1.86 us (1%)
    pallas_call x1, Pallas kernels, per_device(): pl.pallas_call(functools.partial(kernel, tokens_all), out_shape=(out, out...  124 us
    unnamed x13, local copies, waits for them, and re-layouts  6.45 us

commit v1 on v0

v1 whole, which is shorter than its diff:
```python
import functools

import jax
import jax.numpy as jnp
from jax import lax
from jax.experimental import pallas as pl
from jax.experimental.pallas import tpu as pltpu
from jax.sharding import PartitionSpec as P

HD = 128
LEVELS = 64
TOKF = 256
NEG = -1e30
LOG2E = 1.4426950408889634
MESH = pl.DeviceIdType.MESH

NT = (((1,), (1,)), ((), ()))
NN = (((1,), (0,)), ((), ()))


def dot(a, b, dims):
    return lax.dot_general(a, b, dims, preferred_element_type=jnp.float32)


def kernel(
    tokens_all, flags, levels,
    q_hbm, k_hbm, v_hbm, o_hbm, c_hbm, w_hbm, gate_hbm,
    dq_hbm, dk_hbm, dv_hbm, dw_hbm,
    w_ref, g_ref, q_ref, o_ref, k_ref, v_ref, c_ref, gate_ref, ot_ref, dacc,
    s1_send, s1_recv, gsum, far_send, far_recv, near_send, near_recv, x_send, x_recv, dw_ref,
    own_k, own_v, h_send, h_recv, dq_ref, dk_ref, dv_ref,
    loc_sem, exo_send, exo_recv, ex_send, ex_recv, ag_send, ag_recv, halo_ssem, halo_rsem,
    s1_ssem, s1_rsem, far_ssem, far_rsem, near_ssem, near_rsem, x_ssem, x_rsem, hg_ssem, hg_rsem, out_sem, dw_sem,
):
    f, h, s = lax.axis_index("frame"), lax.axis_index("head"), lax.axis_index("fsdp")
    nf = 8
    nh = 8
    y, c = f // 2, f % 2
    xh, z = h // 4, h % 4
    zp, zm = (z + 1) % 4, (z + 3) % 4
    right, left = (f + 1) % nf, (f + 7) % nf
    up, down = (f + 2) % nf, (f + 6) % nf
    pair = 2 * y + 1 - c
    rows = 32
    wid = 640
    heads = 5
    inv_root = HD ** (-0.5)

    def col(j):
        return pl.ds(pl.multiple_of(j * wid, 128), wid)

    def rows_of(n):
        return pl.ds(pl.multiple_of(n * rows, 32), rows)

    my_rows = rows_of(h)

    def chunk_of(t2):
        t = t2 // 2
        step = jnp.where(t == 0, 2, jnp.where(t == 1, 1, jnp.where(t == 2, 3, 0)))
        yt = (y + step) % 4
        return 2 * yt + jnp.where(t2 % 2 == 0, 1 - c, c)

    def head_cols(d, hh):
        return pl.ds(pl.multiple_of(d * wid + hh * HD, 128), HD)

    c_copy = pltpu.make_async_copy(c_hbm, c_ref, loc_sem.at[0])
    gate_copy = pltpu.make_async_copy(gate_hbm, gate_ref, loc_sem.at[1])
    o_copy = pltpu.make_async_copy(o_hbm.at[:, :, col(h)], o_ref.at[:, my_rows, :], loc_sem.at[2])
    w_copy = pltpu.make_async_copy(w_hbm, w_ref, loc_sem.at[3])

    def own_copy(i, hh):
        src, dst = (
            (k_hbm, k_ref.at[hh, pl.ds(1, 2), my_rows, :]),
            (v_hbm, v_ref.at[hh, pl.ds(1, 2), my_rows, :]),
            (q_hbm, q_ref.at[hh, :, my_rows, :]),
        )[i]
        return pltpu.make_async_copy(src.at[:, :, head_cols(h, hh)], dst, ex_recv.at[hh, i, 0])

    barrier = pltpu.get_barrier_semaphore()
    for p in range(1, nh):
        pl.semaphore_signal(barrier, inc=1, device_id={"head": (h + p) % nh}, device_id_type=MESH)
    for other in (right, left, up, down):
        pl.semaphore_signal(barrier, inc=1, device_id={"frame": other}, device_id_type=MESH)
    pl.semaphore_signal(barrier, inc=1, device_id={"fsdp": 1 - s}, device_id_type=MESH)
    c_copy.start()
    gate_copy.start()
    o_copy.start()
    w_copy.start()

    @pl.loop(0, heads)
    def _(hh):
        for i in range(3):
            own_copy(i, hh).start()

    c_copy.wait()
    gate_copy.wait()
    for lf in range(2):
        gain = gate_ref[pl.ds(levels[lf], 1), :]
        g_ref[lf, my_rows, :] = (c_ref[lf].astype(jnp.float32) * gain).astype(jnp.bfloat16)
    pl.semaphore_wait(barrier, nh - 1 + 5)

    def o_exchange(p):
        d = (h + p) % nh
        return pltpu.make_async_remote_copy(
            src_ref=o_hbm.at[:, :, col(d)], dst_ref=o_ref.at[:, my_rows, :],
            send_sem=exo_send.at[p], recv_sem=exo_recv.at[p],
            device_id={"head": d}, device_id_type=MESH,
        )

    def exchange(i, hh, p):
        d = (h + p) % nh
        src, dst = (
            (k_hbm, k_ref.at[hh, pl.ds(1, 2), my_rows, :]),
            (v_hbm, v_ref.at[hh, pl.ds(1, 2), my_rows, :]),
            (q_hbm, q_ref.at[hh, :, my_rows, :]),
        )[i]
        return pltpu.make_async_remote_copy(
            src_ref=src.at[:, :, head_cols(d, hh)], dst_ref=dst,
            send_sem=ex_send.at[hh, i, p], recv_sem=ex_recv.at[hh, i, p],
            device_id={"head": d}, device_id_type=MESH,
        )

    def part(t2, n, half, idx, xt, zt):
        cols = col(chunk_of(t2))
        ref = g_ref.at[:, rows_of(n), cols] if half is None else g_ref.at[half, rows_of(n), cols]
        return pltpu.make_async_remote_copy(
            src_ref=ref, dst_ref=ref, send_sem=ag_send.at[t2, idx], recv_sem=ag_recv.at[t2, idx],
            device_id={"head": xt * 4 + zt}, device_id_type=MESH,
        )

    def gather(t2, idx):
        xo = 1 - xh
        return (
            lambda: part(t2, h, None, 0, xh, zp),
            lambda: part(t2, h, None, 1, xh, zm),
            lambda: part(t2, xh * 4 + zm, None, 2, xo, z),
            lambda: part(t2, xh * 4 + zp, None, 3, xo, z),
            lambda: part(t2, xh * 4 + zm, 0, 4, xh, zp),
            lambda: part(t2, xh * 4 + zp, 1, 5, xh, zm),
            lambda: part(t2, xo * 4 + zm, 0, 6, xh, zp),
            lambda: part(t2, xo * 4 + zm, 0, 7, xh, zm),
            lambda: part(t2, xo * 4 + zp, 1, 8, xh, zp),
            lambda: part(t2, xo * 4 + zp, 1, 9, xh, zm),
        )[idx]()

    def stage1(t2):
        gather(t2, 0).start()
        gather(t2, 1).start()

    def stage2(t2):
        gather(t2, 0).wait_recv()
        gather(t2, 2).start()
        gather(t2, 4).start()
        gather(t2, 1).wait_recv()
        gather(t2, 3).start()
        gather(t2, 5).start()

    def stage3(t2):
        gather(t2, 2).wait_recv()
        gather(t2, 6).start()
        gather(t2, 7).start()
        gather(t2, 3).wait_recv()
        gather(t2, 8).start()
        gather(t2, 9).start()

    order = (4, 2, 6, 1, 7, 3, 5)
    stage1(0)
    stage1(1)
    for p in order:
        o_exchange(p).start()

    def halo(i, hh, which):
        ref = (k_ref, v_ref)[i]
        return pltpu.make_async_remote_copy(
            src_ref=ref.at[hh, 2 if which == 0 else 1], dst_ref=ref.at[hh, 0 if which == 0 else 3],
            send_sem=halo_ssem.at[i, hh, which], recv_sem=halo_rsem.at[i, hh, which],
            device_id={"frame": right if which == 0 else left}, device_id_type=MESH,
        )

    def s1(t):
        return pltpu.make_async_remote_copy(
            src_ref=s1_send.at[t], dst_ref=s1_recv.at[t], send_sem=s1_ssem.at[t], recv_sem=s1_rsem.at[t],
            device_id={"frame": pair}, device_id_type=MESH,
        )

    def far(i):
        return pltpu.make_async_remote_copy(
            src_ref=far_send.at[i], dst_ref=far_recv.at[i], send_sem=far_ssem.at[i], recv_sem=far_rsem.at[i],
            device_id={"frame": up if i == 0 else down}, device_id_type=MESH,
        )

    def near(i):
        return pltpu.make_async_remote_copy(
            src_ref=near_send.at[i], dst_ref=near_recv.at[i], send_sem=near_ssem.at[i], recv_sem=near_rsem.at[i],
            device_id={"frame": up if i == 0 else down}, device_id_type=MESH,
        )

    def one_chunk(t2):
        for idx in range(4, 10):
            gather(t2, idx).wait_recv()
        cols = col(chunk_of(t2))
        rhs = g_ref[:, :, cols].reshape(2 * TOKF, wid)
        dacc[...] += dot(rhs, w_ref[:, cols], NT)
        return dot(ot_ref[...], rhs, NN) * (1.0 / tokens_all)

    def finish_near(i):
        far(i).wait_recv()
        half = pl.ds(320 * i, 320)
        rest = pl.ds(320 * (1 - i), 320)
        near_send[i, half, :] = (gsum[1 + i, half, :] + far_recv[i].astype(jnp.float32)).astype(jnp.bfloat16)
        near_send[i, rest, :] = gsum[1 + i, rest, :].astype(jnp.bfloat16)
        near(i).start()

    @pl.loop(0, 5)
    def _(tt):
        t = tt - 1

        @pl.when(tt < 3)
        def _():
            stage1(2 * tt + 2)

        @pl.when(tt < 4)
        def _():
            stage2(2 * tt)

        @pl.when(tt >= 1)
        def _():
            stage3(2 * tt - 1)

        @pl.when(tt == 0)
        def _():
            o_copy.wait()
            for p in range(1, nh):
                o_exchange(p).wait_recv()
            for lf in range(2):
                ot_ref[:, pl.ds(lf * TOKF, TOKF)] = o_ref[lf].astype(jnp.float32).T.astype(jnp.bfloat16)
            w_copy.wait()
            dacc[...] = jnp.zeros_like(dacc)

        @pl.when(tt == 4)
        def _():
            @pl.loop(0, heads)
            def _(hh):
                for i in range(3):
                    for p in order:
                        exchange(i, hh, p).start()

        @pl.when(tt >= 1)
        def _():
            s1_send[t] = one_chunk(2 * t).astype(jnp.bfloat16)
            s1(t).start()

        @pl.when(tt < 3)
        def _():
            stage1(2 * tt + 3)

        @pl.when(tt < 4)
        def _():
            stage2(2 * tt + 1)
            stage3(2 * tt)

        @pl.when(t == 2)
        def _():
            finish_near(0)

        @pl.when(t == 3)
        def _():
            finish_near(1)

        @pl.when(tt >= 1)
        def _():
            gsum[t] = one_chunk(2 * t + 1)
            s1(t).wait_recv()
            gsum[t] += s1_recv[t].astype(jnp.float32)

        @pl.when(t == 0)
        def _():
            for i in range(2):
                far_send[i] = gsum[0, pl.ds(320 * i, 320), :].astype(jnp.bfloat16)
                far(i).start()

    x_copy = pltpu.make_async_remote_copy(
        src_ref=x_send, dst_ref=x_recv, send_sem=x_ssem, recv_sem=x_rsem,
        device_id={"fsdp": 1 - s}, device_id_type=MESH,
    )

    def halo_grad(i, hh):
        return pltpu.make_async_remote_copy(
            src_ref=h_send.at[i, hh], dst_ref=h_recv.at[i, hh], send_sem=hg_ssem.at[i, hh], recv_sem=hg_rsem.at[i, hh],
            device_id={"frame": left if i == 0 else right}, device_id_type=MESH,
        )

    def bias_of(fr, column, offset):
        target = fr + offset
        inside = (target >= 0) & (target < 2 * nf)
        chosen = flags[column, fr] == 1
        first = jnp.where(inside, 0.0, NEG).astype(jnp.float32)
        second = jnp.where(inside & chosen, 0.0, NEG).astype(jnp.float32)
        return first, second

    def attend(hh):
        hs = pl.ds(pl.multiple_of(hh * HD, 128), HD)
        gk = []
        gv = []
        for lf in range(2):
            q = q_ref[hh, lf]
            parts = []
            for w in range(3):
                sc = dot(k_ref[hh, lf + w], q, NT) * (inv_root * LOG2E)
                if w == 1:
                    parts.append(sc)
                else:
                    first, second = bias_of(2 * f + lf, 0 if w == 0 else 1, w - 1)
                    parts.append(jnp.concatenate([sc[:128] + first, sc[128:] + second], axis=0))
            m = functools.reduce(jnp.maximum, [jnp.max(x, axis=0, keepdims=True) for x in parts])
            parts = [jnp.exp2(x - m) for x in parts]
            total = functools.reduce(jnp.add, [jnp.sum(x, axis=0, keepdims=True) for x in parts])
            inv = 1.0 / total
            d_out = dacc[pl.ds(lf * TOKF, TOKF), hs].astype(jnp.bfloat16)
            delta = jnp.sum(
                (d_out.astype(jnp.float32) * o_ref[lf, :, hs].astype(jnp.float32)).T, axis=0, keepdims=True
            )
            dq_t = jnp.zeros((HD, TOKF), jnp.float32)
            for w in range(3):
                pr = parts[w] * inv
                dp = dot(v_ref[hh, lf + w], d_out, NT)
                ds = (pr * (dp - delta)).astype(jnp.bfloat16)
                gv.append(dot(pr.astype(jnp.bfloat16), d_out, NN))
                gk.append(dot(ds, q, NN) * inv_root)
                kt = k_ref[hh, lf + w].astype(jnp.float32).T.astype(jnp.bfloat16)
                dq_t = dq_t + dot(kt, ds, NN)
            dq_ref[hh, lf] = (dq_t.T * inv_root).astype(jnp.bfloat16)
        h_send[0, hh, 0] = gk[0].astype(jnp.bfloat16)
        h_send[0, hh, 1] = gv[0].astype(jnp.bfloat16)
        h_send[1, hh, 0] = gk[5].astype(jnp.bfloat16)
        h_send[1, hh, 1] = gv[5].astype(jnp.bfloat16)
        halo_grad(0, hh).start()
        halo_grad(1, hh).start()
        own_k[hh, 0] = gk[1] + gk[3]
        own_k[hh, 1] = gk[2] + gk[4]
        own_v[hh, 0] = gv[1] + gv[3]
        own_v[hh, 1] = gv[2] + gv[4]

    def out_copy(i, hh):
        hs = pl.ds(pl.multiple_of(hh * HD, 128), HD)
        src, dst = ((dq_ref, dq_hbm), (dk_ref, dk_hbm), (dv_ref, dv_hbm))[i]
        return pltpu.make_async_copy(src.at[hh], dst.at[:, :, hs], out_sem.at[i, hh])

    def finish(hh):
        halo_grad(0, hh).wait_recv()
        halo_grad(1, hh).wait_recv()
        dk_ref[hh, 0] = (own_k[hh, 0] + h_recv[1, hh, 0].astype(jnp.float32)).astype(jnp.bfloat16)
        dk_ref[hh, 1] = (own_k[hh, 1] + h_recv[0, hh, 0].astype(jnp.float32)).astype(jnp.bfloat16)
        dv_ref[hh, 0] = (own_v[hh, 0] + h_recv[1, hh, 1].astype(jnp.float32)).astype(jnp.bfloat16)
        dv_ref[hh, 1] = (own_v[hh, 1] + h_recv[0, hh, 1].astype(jnp.float32)).astype(jnp.bfloat16)
        for i in range(3):
            out_copy(i, hh).start()

    @pl.loop(0, heads + 2)
    def _(n):
        @pl.when(n < heads)
        def _():
            for i in range(2):
                own_copy(i, n).wait()
                for p in range(1, nh):
                    exchange(i, n, p).wait_recv()
                halo(i, n, 0).start()
                halo(i, n, 1).start()

        @pl.when(n == heads)
        def _():
            near(0).wait_recv()
            near(1).wait_recv()
            gsum[3] += near_recv[0].astype(jnp.float32) + near_recv[1].astype(jnp.float32)
            x_send[...] = gsum[3, :, pl.ds(pl.multiple_of(256 * (1 - s), 128), 384)].astype(jnp.bfloat16)
            x_copy.start()

        @pl.when((n >= 1) & (n <= heads))
        def _():
            hh = n - 1
            own_copy(2, hh).wait()
            for p in range(1, nh):
                exchange(2, hh, p).wait_recv()
            for i in range(2):
                halo(i, hh, 0).wait_recv()
                halo(i, hh, 1).wait_recv()
            attend(hh)

        @pl.when(n >= 2)
        def _():
            finish(n - 2)

    x_copy.wait_recv()
    final = (gsum[3, :, pl.ds(pl.multiple_of(256 * s, 128), 384)] + x_recv[...].astype(jnp.float32)).T
    dw_ref[...] = jnp.where(s == 0, final[:320], final[64:384])
    dw_out = pltpu.make_async_copy(dw_ref, dw_hbm, dw_sem)
    dw_out.start()

    for p in range(1, nh):
        o_exchange(p).wait_send()

    @pl.loop(0, heads)
    def _(hh):
        for i in range(3):
            for p in range(1, nh):
                exchange(i, hh, p).wait_send()
            out_copy(i, hh).wait()
        for i in range(2):
            halo(i, hh, 0).wait_send()
            halo(i, hh, 1).wait_send()
            halo_grad(i, hh).wait_send()

    @pl.loop(0, 8)
    def _(t2):
        for idx in range(10):
            gather(t2, idx).wait_send()

    for i in range(2):
        far(i).wait_send()
        near(i).wait_send()

    @pl.loop(0, 4)
    def _(t):
        s1(t).wait_send()

    x_copy.wait_send()
    dw_out.wait()


def per_device(
    queries, key_rows, value_rows, saved_out, cotangent, out_weight, gate_table, levels, reach_flags
):
    frame_dev = queries.shape[1]
    tokens_all = lax.axis_size("fsdp") * frame_dev * lax.axis_size("frame") * TOKF
    bf, f32 = jnp.bfloat16, jnp.float32
    vm = pltpu.VMEM
    dma = pltpu.SemaphoreType.DMA
    hbm = pl.BlockSpec(memory_space=pl.ANY)
    smem = pl.BlockSpec(memory_space=pltpu.SMEM)
    out = jax.ShapeDtypeStruct((2, TOKF, 640), bf)
    dq, dk, dv, dw = pl.pallas_call(
        functools.partial(kernel, tokens_all),
        out_shape=(out, out, out, jax.ShapeDtypeStruct((320, 640), f32)),
        in_specs=[smem, smem] + [hbm] * 7,
        out_specs=(hbm,) * 4,
        scratch_shapes=[
            vm((640, 5120), bf),
            vm((2, TOKF, 5120), bf),
            vm((5, 2, TOKF, HD), bf),
            vm((2, TOKF, 640), bf),
            vm((5, 4, TOKF, HD), bf),
            vm((5, 4, TOKF, HD), bf),
            vm((2, 32, 5120), bf),
            vm((LEVELS, 5120), f32),
            vm((640, 2 * TOKF), bf),
            vm((2 * TOKF, 640), f32),
            vm((4, 640, 640), bf),
            vm((4, 640, 640), bf),
            vm((4, 640, 640), f32),
            vm((2, 320, 640), bf),
            vm((2, 320, 640), bf),
            vm((2, 640, 640), bf),
            vm((2, 640, 640), bf),
            vm((640, 384), bf),
            vm((640, 384), bf),
            vm((320, 640), f32),
            vm((5, 2, TOKF, HD), f32),
            vm((5, 2, TOKF, HD), f32),
            vm((2, 5, 2, TOKF, HD), bf),
            vm((2, 5, 2, TOKF, HD), bf),
            vm((5, 2, TOKF, HD), bf),
            vm((5, 2, TOKF, HD), bf),
            vm((5, 2, TOKF, HD), bf),
            dma((4,)),
            dma((8,)), dma((8,)),
            dma((5, 3, 8)), dma((5, 3, 8)),
            dma((8, 10)), dma((8, 10)),
            dma((2, 5, 2)), dma((2, 5, 2)),
            dma((4,)), dma((4,)),
            dma((2,)), dma((2,)),
            dma((2,)), dma((2,)),
            dma(()), dma(()),
            dma((2, 5)), dma((2, 5)),
            dma((3, 5)), dma(()),
        ],
        compiler_params=pltpu.CompilerParams(
            collective_id=0, has_side_effects=True, vmem_limit_bytes=67043328
        ),
        name="window_backward",
    )(
        reach_flags.T, levels, queries[0], key_rows[0], value_rows[0], saved_out[0], cotangent[0], out_weight, gate_table
    )
    return (dq[None], dk[None], dv[None], dw.T)


def solution(mesh):
    in_specs = (
        P("fsdp", "frame", "head", None),
        P("fsdp", "frame", "head", None),
        P("fsdp", "frame", "head", None),
        P("fsdp", "frame", "head", None),
        P("fsdp", "frame", "head", None),
        P("head", None),
        P(),
        P("frame"),
        P(),
    )
    out_specs = (
        P("fsdp", "frame", None, "head"),
        P("fsdp", "frame", None, "head"),
        P("fsdp", "frame", None, "head"),
        P("head", ("frame", "fsdp")),
    )
    return jax.shard_map(
        per_device, mesh=mesh, in_specs=in_specs, out_specs=out_specs, check_vma=False
    )
```

time: 134 us -> 114 us (0.85)
  the two profiles are of different devices: /device:TPU:6 before, /device:TPU:0 now
where the time goes in v1:
time: 114 us; the launch traced here: 113 us
  Pallas kernels  105 us (92%)
  local copies, waits for them, and re-layouts  8.03 us (7%)
    pallas_call x1, Pallas kernels, per_device(): pl.pallas_call(functools.partial(kernel, tokens_all), out_shape=(out, out...  105 us
    unnamed x4, local copies, waits for them, and re-layouts  8.03 us

profile of v1, /device:TPU:0, one launch (start us, length us, event | category | flops | bytes accessed | tf_op | source)
XLA Modules:
  0.0 113.3 jit_solution(16098683681848524863)
XLA Ops:
  0.6 104.7 %window_backward.1 = (bf16[2,256,640]{2,1,0:T(8,128)(2,1)}, bf16[2,256,640]{2,1,0:T(8,128)(2,1)}, bf16[2,256,640]{2,1,0:T(8,128)(2,1)}, f32[320,640]{1,0:T(8,128)}) custom-call(s32[2,16]{1,0:T(2,128)} %bitcast.19, s32[2]{0:T(128)} %levels.1, bf16[2,32,5120]{2,1,0:T(8,128)(2,1)} %bitcast.11, bf16[2,32,5120]{2,1,0:T(8,128)(2,1)} %bitcast.12, ...), custom_call_target="tpu_custom_call" | custom-call | tf_op jit(solution)/shard_map/window_backward/pallas_call | solution.py:441
  105.3 2.0 %copy.17 = bf16[1,2,256,640]{3,2,1,0:T(8,128)(2,1)} copy(bf16[1,2,256,640]{3,2,1,0:T(8,128)(2,1)} %bitcast.18) | data formatting | bytes 1310720
  107.3 2.0 %copy.18 = bf16[1,2,256,640]{3,2,1,0:T(8,128)(2,1)} copy(bf16[1,2,256,640]{3,2,1,0:T(8,128)(2,1)} %bitcast.17) | data formatting | bytes 1310720
  109.3 2.0 %copy.19 = bf16[1,2,256,640]{3,2,1,0:T(8,128)(2,1)} copy(bf16[1,2,256,640]{3,2,1,0:T(8,128)(2,1)} %bitcast.16) | data formatting | bytes 1310720
  111.3 2.1 %copy.20 = f32[640,320]{0,1:T(8,128)} copy(f32[640,320]{0,1:T(8,128)} %bitcast.10) | data formatting | bytes 1638400

commit v2 on v1

--- a/solution.py
+++ b/solution.py
@@ -25,12 +25,12 @@
 def kernel(
     tokens_all, flags, levels,
     q_hbm, k_hbm, v_hbm, o_hbm, c_hbm, w_hbm, gate_hbm,
-    dq_hbm, dk_hbm, dv_hbm, dw_hbm,
+    dq_ref, dk_ref, dv_ref, dw_ref,
     w_ref, g_ref, q_ref, o_ref, k_ref, v_ref, c_ref, gate_ref, ot_ref, dacc,
-    s1_send, s1_recv, gsum, far_send, far_recv, near_send, near_recv, x_send, x_recv, dw_ref,
-    own_k, own_v, h_send, h_recv, dq_ref, dk_ref, dv_ref,
-    loc_sem, exo_send, exo_recv, ex_send, ex_recv, ag_send, ag_recv, halo_ssem, halo_rsem,
-    s1_ssem, s1_rsem, far_ssem, far_rsem, near_ssem, near_rsem, x_ssem, x_rsem, hg_ssem, hg_rsem, out_sem, dw_sem,
+    s1_send, s1_recv, gsum, far_send, far_recv, near_send, near_recv, x_send, x_recv,
+    own_k, own_v, h_send, h_recv,
+    loc_sem, w_sem, exo_send, exo_recv, ex_send, ex_recv, ag_send, ag_recv, halo_ssem, halo_rsem,
+    s1_ssem, s1_rsem, far_ssem, far_rsem, near_ssem, near_rsem, x_ssem, x_rsem, hg_ssem, hg_rsem,
 ):
     f, h, s = lax.axis_index("frame"), lax.axis_index("head"), lax.axis_index("fsdp")
     nf = 8
@@ -54,11 +54,15 @@
 
     my_rows = rows_of(h)
 
-    def chunk_of(t2):
-        t = t2 // 2
-        step = jnp.where(t == 0, 2, jnp.where(t == 1, 1, jnp.where(t == 2, 3, 0)))
-        yt = (y + step) % 4
-        return 2 * yt + jnp.where(t2 % 2 == 0, 1 - c, c)
+    def pieces(t2):
+        core = 1 - c if t2 % 2 == 0 else c
+        ahead, back = ((y + 1) % 4 * 2 + core) * wid, ((y + 3) % 4 * 2 + core) * wid
+        return (
+            ((((y + 2) % 4 * 2 + core) * wid, 0, wid),),
+            ((ahead, 0, 384), (back, 384, 256)),
+            ((ahead + 384, 0, 256), (back + 256, 256, 384)),
+            (((y * 2 + core) * wid, 0, wid),),
+        )[t2 // 2]
 
     def head_cols(d, hh):
         return pl.ds(pl.multiple_of(d * wid + hh * HD, 128), HD)
@@ -66,7 +70,14 @@
     c_copy = pltpu.make_async_copy(c_hbm, c_ref, loc_sem.at[0])
     gate_copy = pltpu.make_async_copy(gate_hbm, gate_ref, loc_sem.at[1])
     o_copy = pltpu.make_async_copy(o_hbm.at[:, :, col(h)], o_ref.at[:, my_rows, :], loc_sem.at[2])
-    w_copy = pltpu.make_async_copy(w_hbm, w_ref, loc_sem.at[3])
+    w_copies = []
+    for t2 in range(8):
+        for k, (start, at, width) in enumerate(pieces(t2)):
+            w_copies.append(
+                pltpu.make_async_copy(
+                    w_hbm.at[:, pl.ds(pl.multiple_of(start, 128), width)], w_ref.at[t2, :, pl.ds(at, width)], w_sem.at[t2, k]
+                )
+            )
 
     def own_copy(i, hh):
         src, dst = (
@@ -85,7 +96,8 @@
     c_copy.start()
     gate_copy.start()
     o_copy.start()
-    w_copy.start()
+    for copy in w_copies:
+        copy.start()
 
     @pl.loop(0, heads)
     def _(hh):
@@ -94,9 +106,12 @@
 
     c_copy.wait()
     gate_copy.wait()
-    for lf in range(2):
-        gain = gate_ref[pl.ds(levels[lf], 1), :]
-        g_ref[lf, my_rows, :] = (c_ref[lf].astype(jnp.float32) * gain).astype(jnp.bfloat16)
+    for t2 in range(8):
+        for start, at, width in pieces(t2):
+            cols = pl.ds(pl.multiple_of(start, 128), width)
+            for lf in range(2):
+                gain = gate_ref[pl.ds(levels[lf], 1), cols]
+                g_ref[t2, lf, my_rows, pl.ds(at, width)] = (c_ref[lf, :, cols].astype(jnp.float32) * gain).astype(jnp.bfloat16)
     pl.semaphore_wait(barrier, nh - 1 + 5)
 
     def o_exchange(p):
@@ -121,8 +136,7 @@
         )
 
     def part(t2, n, half, idx, xt, zt):
-        cols = col(chunk_of(t2))
-        ref = g_ref.at[:, rows_of(n), cols] if half is None else g_ref.at[half, rows_of(n), cols]
+        ref = g_ref.at[t2, :, rows_of(n)] if half is None else g_ref.at[t2, half, rows_of(n)]
         return pltpu.make_async_remote_copy(
             src_ref=ref, dst_ref=ref, send_sem=ag_send.at[t2, idx], recv_sem=ag_recv.at[t2, idx],
             device_id={"head": xt * 4 + zt}, device_id_type=MESH,
@@ -164,8 +178,8 @@
         gather(t2, 9).start()
 
     order = (4, 2, 6, 1, 7, 3, 5)
-    stage1(0)
-    stage1(1)
+    for t2 in range(4):
+        stage1(t2)
     for p in order:
         o_exchange(p).start()
 
@@ -183,49 +197,81 @@
             device_id={"frame": pair}, device_id_type=MESH,
         )
 
+    far_cols = (pl.ds(0, 384), pl.ds(384, 256))
+    near_cols = ((pl.ds(0, 384), pl.ds(384, 256)), (pl.ds(0, 256), pl.ds(256, 384)))
+
     def far(i):
         return pltpu.make_async_remote_copy(
-            src_ref=far_send.at[i], dst_ref=far_recv.at[i], send_sem=far_ssem.at[i], recv_sem=far_rsem.at[i],
+            src_ref=far_send.at[:, far_cols[i]], dst_ref=far_recv.at[:, far_cols[i]],
+            send_sem=far_ssem.at[i], recv_sem=far_rsem.at[i],
             device_id={"frame": up if i == 0 else down}, device_id_type=MESH,
         )
 
-    def near(i):
-        return pltpu.make_async_remote_copy(
-            src_ref=near_send.at[i], dst_ref=near_recv.at[i], send_sem=near_ssem.at[i], recv_sem=near_rsem.at[i],
+    def near(i, r):
+        return pltpu.make_async_remote_copy(
+            src_ref=near_send.at[i, :, near_cols[i][r]], dst_ref=near_recv.at[i, :, near_cols[i][r]],
+            send_sem=near_ssem.at[i, r], recv_sem=near_rsem.at[i, r],
             device_id={"frame": up if i == 0 else down}, device_id_type=MESH,
         )
 
     def one_chunk(t2):
         for idx in range(4, 10):
             gather(t2, idx).wait_recv()
-        cols = col(chunk_of(t2))
-        rhs = g_ref[:, :, cols].reshape(2 * TOKF, wid)
-        dacc[...] += dot(rhs, w_ref[:, cols], NT)
+        rhs = g_ref[t2].reshape(2 * TOKF, wid)
+        dacc[...] += dot(rhs, w_ref[t2], NT)
         return dot(ot_ref[...], rhs, NN) * (1.0 / tokens_all)
 
-    def finish_near(i):
-        far(i).wait_recv()
-        half = pl.ds(320 * i, 320)
-        rest = pl.ds(320 * (1 - i), 320)
-        near_send[i, half, :] = (gsum[1 + i, half, :] + far_recv[i].astype(jnp.float32)).astype(jnp.bfloat16)
-        near_send[i, rest, :] = gsum[1 + i, rest, :].astype(jnp.bfloat16)
-        near(i).start()
+    def send_near(i, r):
+        if (i, r) == (0, 0):
+            far(0).wait_recv()
+            near_send[0, :, pl.ds(0, 384)] = (gsum[1, :, pl.ds(0, 384)] + far_recv[:, pl.ds(0, 384)].astype(jnp.float32)).astype(
+                jnp.bfloat16
+            )
+        elif (i, r) == (1, 0):
+            near_send[1, :, pl.ds(0, 256)] = gsum[1, :, pl.ds(384, 256)].astype(jnp.bfloat16)
+        elif (i, r) == (0, 1):
+            near_send[0, :, pl.ds(384, 256)] = gsum[2, :, pl.ds(0, 256)].astype(jnp.bfloat16)
+        else:
+            far(1).wait_recv()
+            near_send[1, :, pl.ds(256, 128)] = gsum[2, :, pl.ds(256, 128)].astype(jnp.bfloat16)
+            near_send[1, :, pl.ds(384, 256)] = (gsum[2, :, pl.ds(384, 256)] + far_recv[:, pl.ds(384, 256)].astype(jnp.float32)).astype(
+                jnp.bfloat16
+            )
+        near(i, r).start()
+
+    def send_head(n):
+        @pl.when(n < heads)
+        def _():
+            for i in range(2):
+                for p in order:
+                    exchange(i, n, p).start()
+
+        @pl.when((n >= 1) & (n <= heads))
+        def _():
+            for p in order:
+                exchange(2, n - 1, p).start()
+
+    def forward(tt, u):
+        @pl.when(tt < 4)
+        def _():
+            stage3(u)
+
+        @pl.when(tt < 3)
+        def _():
+            stage2(u + 2)
+
+        @pl.when(tt < 2)
+        def _():
+            stage1(u + 4)
+
+    stage2(0)
+    stage2(1)
 
     @pl.loop(0, 5)
     def _(tt):
         t = tt - 1
 
-        @pl.when(tt < 3)
-        def _():
-            stage1(2 * tt + 2)
-
-        @pl.when(tt < 4)
-        def _():
-            stage2(2 * tt)
-
-        @pl.when(tt >= 1)
-        def _():
-            stage3(2 * tt - 1)
+        forward(tt, 2 * tt)
 
         @pl.when(tt == 0)
         def _():
@@ -234,38 +280,25 @@
                 o_exchange(p).wait_recv()
             for lf in range(2):
                 ot_ref[:, pl.ds(lf * TOKF, TOKF)] = o_ref[lf].astype(jnp.float32).T.astype(jnp.bfloat16)
-            w_copy.wait()
+            for copy in w_copies:
+                copy.wait()
             dacc[...] = jnp.zeros_like(dacc)
-
-        @pl.when(tt == 4)
-        def _():
-            @pl.loop(0, heads)
-            def _(hh):
-                for i in range(3):
-                    for p in order:
-                        exchange(i, hh, p).start()
 
         @pl.when(tt >= 1)
         def _():
             s1_send[t] = one_chunk(2 * t).astype(jnp.bfloat16)
             s1(t).start()
 
-        @pl.when(tt < 3)
-        def _():
-            stage1(2 * tt + 3)
-
-        @pl.when(tt < 4)
-        def _():
-            stage2(2 * tt + 1)
-            stage3(2 * tt)
+        forward(tt, 2 * tt + 1)
+
+        @pl.when(tt == 3)
+        def _():
+            for n in range(3):
+                send_head(n)
 
         @pl.when(t == 2)
         def _():
-            finish_near(0)
-
-        @pl.when(t == 3)
-        def _():
-            finish_near(1)
+            send_near(0, 0)
 
         @pl.when(tt >= 1)
         def _():
@@ -276,13 +309,31 @@
         @pl.when(t == 0)
         def _():
             for i in range(2):
-                far_send[i] = gsum[0, pl.ds(320 * i, 320), :].astype(jnp.bfloat16)
+                far_send[:, far_cols[i]] = gsum[0, :, far_cols[i]].astype(jnp.bfloat16)
                 far(i).start()
+
+        @pl.when(t == 1)
+        def _():
+            send_near(1, 0)
+
+        @pl.when(t == 2)
+        def _():
+            send_near(0, 1)
+            send_near(1, 1)
 
     x_copy = pltpu.make_async_remote_copy(
         src_ref=x_send, dst_ref=x_recv, send_sem=x_ssem, recv_sem=x_rsem,
         device_id={"fsdp": 1 - s}, device_id_type=MESH,
     )
+
+    def own_block():
+        for i in range(2):
+            for r in range(2):
+                near(i, r).wait_recv()
+        total = gsum[3] + near_recv[0].astype(jnp.float32) + near_recv[1].astype(jnp.float32)
+        gsum[0] = total.T
+        x_send[...] = gsum[0, pl.ds(pl.multiple_of(320 * (1 - s), 64), 320), :].astype(jnp.bfloat16)
+        x_copy.start()
 
     def halo_grad(i, hh):
         return pltpu.make_async_remote_copy(
@@ -300,8 +351,6 @@
 
     def attend(hh):
         hs = pl.ds(pl.multiple_of(hh * HD, 128), HD)
-        gk = []
-        gv = []
         for lf in range(2):
             q = q_ref[hh, lf]
             parts = []
@@ -321,40 +370,35 @@
                 (d_out.astype(jnp.float32) * o_ref[lf, :, hs].astype(jnp.float32)).T, axis=0, keepdims=True
             )
             dq_t = jnp.zeros((HD, TOKF), jnp.float32)
-            for w in range(3):
+            for w in (0, 1, 2) if lf == 0 else (2, 1, 0):
                 pr = parts[w] * inv
                 dp = dot(v_ref[hh, lf + w], d_out, NT)
                 ds = (pr * (dp - delta)).astype(jnp.bfloat16)
-                gv.append(dot(pr.astype(jnp.bfloat16), d_out, NN))
-                gk.append(dot(ds, q, NN) * inv_root)
+                gv = dot(pr.astype(jnp.bfloat16), d_out, NN)
+                gk = dot(ds, q, NN) * inv_root
+                slot = lf + w
+                if slot in (0, 3):
+                    h_send[slot // 3, hh, 0] = gk.astype(jnp.bfloat16)
+                    h_send[slot // 3, hh, 1] = gv.astype(jnp.bfloat16)
+                    halo_grad(slot // 3, hh).start()
+                elif lf == 0:
+                    own_k[hh, slot - 1] = gk
+                    own_v[hh, slot - 1] = gv
+                else:
+                    own_k[hh, slot - 1] += gk
+                    own_v[hh, slot - 1] += gv
                 kt = k_ref[hh, lf + w].astype(jnp.float32).T.astype(jnp.bfloat16)
                 dq_t = dq_t + dot(kt, ds, NN)
-            dq_ref[hh, lf] = (dq_t.T * inv_root).astype(jnp.bfloat16)
-        h_send[0, hh, 0] = gk[0].astype(jnp.bfloat16)
-        h_send[0, hh, 1] = gv[0].astype(jnp.bfloat16)
-        h_send[1, hh, 0] = gk[5].astype(jnp.bfloat16)
-        h_send[1, hh, 1] = gv[5].astype(jnp.bfloat16)
-        halo_grad(0, hh).start()
-        halo_grad(1, hh).start()
-        own_k[hh, 0] = gk[1] + gk[3]
-        own_k[hh, 1] = gk[2] + gk[4]
-        own_v[hh, 0] = gv[1] + gv[3]
-        own_v[hh, 1] = gv[2] + gv[4]
-
-    def out_copy(i, hh):
+            dq_ref[lf, :, hs] = (dq_t.T * inv_root).astype(jnp.bfloat16)
+
+    def finish(hh):
         hs = pl.ds(pl.multiple_of(hh * HD, 128), HD)
-        src, dst = ((dq_ref, dq_hbm), (dk_ref, dk_hbm), (dv_ref, dv_hbm))[i]
-        return pltpu.make_async_copy(src.at[hh], dst.at[:, :, hs], out_sem.at[i, hh])
-
-    def finish(hh):
         halo_grad(0, hh).wait_recv()
         halo_grad(1, hh).wait_recv()
-        dk_ref[hh, 0] = (own_k[hh, 0] + h_recv[1, hh, 0].astype(jnp.float32)).astype(jnp.bfloat16)
-        dk_ref[hh, 1] = (own_k[hh, 1] + h_recv[0, hh, 0].astype(jnp.float32)).astype(jnp.bfloat16)
-        dv_ref[hh, 0] = (own_v[hh, 0] + h_recv[1, hh, 1].astype(jnp.float32)).astype(jnp.bfloat16)
-        dv_ref[hh, 1] = (own_v[hh, 1] + h_recv[0, hh, 1].astype(jnp.float32)).astype(jnp.bfloat16)
-        for i in range(3):
-            out_copy(i, hh).start()
+        dk_ref[0, :, hs] = (own_k[hh, 0] + h_recv[1, hh, 0].astype(jnp.float32)).astype(jnp.bfloat16)
+        dk_ref[1, :, hs] = (own_k[hh, 1] + h_recv[0, hh, 0].astype(jnp.float32)).astype(jnp.bfloat16)
+        dv_ref[0, :, hs] = (own_v[hh, 0] + h_recv[1, hh, 1].astype(jnp.float32)).astype(jnp.bfloat16)
+        dv_ref[1, :, hs] = (own_v[hh, 1] + h_recv[0, hh, 1].astype(jnp.float32)).astype(jnp.bfloat16)
 
     @pl.loop(0, heads + 2)
     def _(n):
@@ -367,13 +411,11 @@
                 halo(i, n, 0).start()
                 halo(i, n, 1).start()
 
-        @pl.when(n == heads)
-        def _():
-            near(0).wait_recv()
-            near(1).wait_recv()
-            gsum[3] += near_recv[0].astype(jnp.float32) + near_recv[1].astype(jnp.float32)
-            x_send[...] = gsum[3, :, pl.ds(pl.multiple_of(256 * (1 - s), 128), 384)].astype(jnp.bfloat16)
-            x_copy.start()
+        @pl.when(n == 3)
+        def _():
+            own_block()
+
+        send_head(n + 3)
 
         @pl.when((n >= 1) & (n <= heads))
         def _():
@@ -391,10 +433,7 @@
             finish(n - 2)
 
     x_copy.wait_recv()
-    final = (gsum[3, :, pl.ds(pl.multiple_of(256 * s, 128), 384)] + x_recv[...].astype(jnp.float32)).T
-    dw_ref[...] = jnp.where(s == 0, final[:320], final[64:384])
-    dw_out = pltpu.make_async_copy(dw_ref, dw_hbm, dw_sem)
-    dw_out.start()
+    dw_ref[...] = gsum[0, pl.ds(pl.multiple_of(320 * s, 64), 320), :] + x_recv[...].astype(jnp.float32)
 
     for p in range(1, nh):
         o_exchange(p).wait_send()
@@ -404,7 +443,6 @@
         for i in range(3):
             for p in range(1, nh):
                 exchange(i, hh, p).wait_send()
-            out_copy(i, hh).wait()
         for i in range(2):
             halo(i, hh, 0).wait_send()
             halo(i, hh, 1).wait_send()
@@ -417,14 +455,21 @@
 
     for i in range(2):
         far(i).wait_send()
-        near(i).wait_send()
+        near(i, 0).wait_send()
+        near(i, 1).wait_send()
+    x_copy.wait_send()
 
     @pl.loop(0, 4)
     def _(t):
         s1(t).wait_send()
 
-    x_copy.wait_send()
-    dw_out.wait()
+
+def write_out(*refs):
+    copies = [pltpu.make_async_copy(refs[i], refs[4 + i], refs[8].at[i]) for i in range(4)]
+    for copy in copies:
+        copy.start()
+    for copy in copies:
+        copy.wait()
 
 
 def per_device(
@@ -437,15 +482,15 @@
     dma = pltpu.SemaphoreType.DMA
     hbm = pl.BlockSpec(memory_space=pl.ANY)
     smem = pl.BlockSpec(memory_space=pltpu.SMEM)
-    out = jax.ShapeDtypeStruct((2, TOKF, 640), bf)
-    dq, dk, dv, dw = pl.pallas_call(
+    out = vm((2, TOKF, 640), bf)
+    held = pl.pallas_call(
         functools.partial(kernel, tokens_all),
-        out_shape=(out, out, out, jax.ShapeDtypeStruct((320, 640), f32)),
+        out_shape=(out, out, out, vm((320, 640), f32)),
         in_specs=[smem, smem] + [hbm] * 7,
-        out_specs=(hbm,) * 4,
+        out_specs=(pl.BlockSpec(memory_space=vm),) * 4,
         scratch_shapes=[
-            vm((640, 5120), bf),
-            vm((2, TOKF, 5120), bf),
+            vm((8, 640, 640), bf),
+            vm((8, 2, TOKF, 640), bf),
             vm((5, 2, TOKF, HD), bf),
             vm((2, TOKF, 640), bf),
             vm((5, 4, TOKF, HD), bf),
@@ -457,39 +502,44 @@
             vm((4, 640, 640), bf),
             vm((4, 640, 640), bf),
             vm((4, 640, 640), f32),
-            vm((2, 320, 640), bf),
-            vm((2, 320, 640), bf),
+            vm((640, 640), bf),
+            vm((640, 640), bf),
             vm((2, 640, 640), bf),
             vm((2, 640, 640), bf),
-            vm((640, 384), bf),
-            vm((640, 384), bf),
-            vm((320, 640), f32),
+            vm((320, 640), bf),
+            vm((320, 640), bf),
             vm((5, 2, TOKF, HD), f32),
             vm((5, 2, TOKF, HD), f32),
             vm((2, 5, 2, TOKF, HD), bf),
             vm((2, 5, 2, TOKF, HD), bf),
-            vm((5, 2, TOKF, HD), bf),
-            vm((5, 2, TOKF, HD), bf),
-            vm((5, 2, TOKF, HD), bf),
-            dma((4,)),
+            dma((3,)), dma((8, 2)),
             dma((8,)), dma((8,)),
             dma((5, 3, 8)), dma((5, 3, 8)),
             dma((8, 10)), dma((8, 10)),
             dma((2, 5, 2)), dma((2, 5, 2)),
             dma((4,)), dma((4,)),
             dma((2,)), dma((2,)),
-            dma((2,)), dma((2,)),
+            dma((2, 2)), dma((2, 2)),
             dma(()), dma(()),
             dma((2, 5)), dma((2, 5)),
-            dma((3, 5)), dma(()),
         ],
         compiler_params=pltpu.CompilerParams(
-            collective_id=0, has_side_effects=True, vmem_limit_bytes=67043328
+            collective_id=0, has_side_effects=True, vmem_limit_bytes=58 * 2**20
         ),
         name="window_backward",
     )(
         reach_flags.T, levels, queries[0], key_rows[0], value_rows[0], saved_out[0], cotangent[0], out_weight, gate_table
     )
+    out = jax.ShapeDtypeStruct((2, TOKF, 640), bf)
+    dq, dk, dv, dw = pl.pallas_call(
+        write_out,
+        out_shape=(out, out, out, jax.ShapeDtypeStruct((320, 640), f32)),
+        in_specs=[pl.BlockSpec(memory_space=vm)] * 4,
+        out_specs=(hbm,) * 4,
+        scratch_shapes=[dma((4,))],
+        compiler_params=pltpu.CompilerParams(vmem_limit_bytes=4 * 2**20),
+        name="write_out",
+    )(*held)
     return (dq[None], dk[None], dv[None], dw.T)
 
 

time: 114 us -> 92.8 us (0.81)
  Pallas kernels: 105 us -> 92 us
  local copies, waits for them, and re-layouts: 8.03 us -> 0 us
    pallas_call x1, Pallas kernels: 105 us -> 90.5 us  [per_device(): pl.pallas_call(functools.partial(kernel, tokens_all), out_shape=(out, out...]
    unnamed x4 -> x0, local copies, waits for them, and re-layouts: 8.03 us -> none
    pallas_call x0 -> x1, Pallas kernels: none -> 1.58 us  [per_device(): pl.pallas_call(write_out, out_shape=(out, out, out, jax.ShapeDtypeStruct(...]
where the time goes in v2:
time: 92.8 us; the launch traced here: 92.7 us
  Pallas kernels  92 us (99%)
    pallas_call x1, Pallas kernels, per_device(): pl.pallas_call(functools.partial(kernel, tokens_all), out_shape=(out, out...  90.5 us

profile of v2, /device:TPU:0, one launch (start us, length us, event | category | flops | bytes accessed | tf_op | source)
XLA Modules:
  0.0 92.7 jit_solution(5484645634233118791)
XLA Ops:
  0.6 90.5 %window_backward.1 = (bf16[2,256,640]{2,1,0:T(8,128)(2,1)S(1)}, bf16[2,256,640]{2,1,0:T(8,128)(2,1)S(1)}, bf16[2,256,640]{2,1,0:T(8,128)(2,1)S(1)}, f32[320,640]{1,0:T(8,128)S(1)}) custom-call(s32[2,16]{1,0:T(2,128)} %bitcast.15, s32[2]{0:T(128)} %levels.1, bf16[2,32,5120]{2,1,0:T(8,128)(2,1)} %bitcast.10, bf16[2,32,5120]{2,1,0:T(8,128)(2,1)} %bitcast.11, ...), custom_call_target="tpu_custom_call" | custom-call | tf_op jit(solution)/shard_map/window_backward/pallas_call | solution.py:486
  91.1 1.6 %write_out.1 = (bf16[2,256,640]{2,1,0:T(8,128)(2,1)}, bf16[2,256,640]{2,1,0:T(8,128)(2,1)}, bf16[2,256,640]{2,1,0:T(8,128)(2,1)}, f32[320,640]{1,0:T(8,128)}) custom-call(bf16[2,256,640]{2,1,0:T(8,128)(2,1)S(1)} %get-tuple-element.12.refs_0_, bf16[2,256,640]{2,1,0:T(8,128)(2,1)S(1)} %get-tuple-element.13.refs_1_, ...), custom_call_target="tpu_custom_call" | custom-call | tf_op jit(solution)/shard_map/write_out/pallas_call | solution.py:534

commit v3 on v2

--- a/solution.py
+++ b/solution.py
@@ -26,10 +26,10 @@
     tokens_all, flags, levels,
     q_hbm, k_hbm, v_hbm, o_hbm, c_hbm, w_hbm, gate_hbm,
     dq_ref, dk_ref, dv_ref, dw_ref,
-    w_ref, g_ref, q_ref, o_ref, k_ref, v_ref, c_ref, gate_ref, ot_ref, dacc,
+    w_ref, g_ref, q_ref, o_ref, k_ref, v_ref, gate_ref, gain_ref, ot_ref, dacc,
     s1_send, s1_recv, gsum, far_send, far_recv, near_send, near_recv, x_send, x_recv,
     own_k, own_v, h_send, h_recv,
-    loc_sem, w_sem, exo_send, exo_recv, ex_send, ex_recv, ag_send, ag_recv, halo_ssem, halo_rsem,
+    loc_sem, w_sem, c_sem, own_sem, exo_send, exo_recv, ex_send, ex_recv, ag_send, ag_recv, ag_part, halo_ssem, halo_rsem,
     s1_ssem, s1_rsem, far_ssem, far_rsem, near_ssem, near_rsem, x_ssem, x_rsem, hg_ssem, hg_rsem,
 ):
     f, h, s = lax.axis_index("frame"), lax.axis_index("head"), lax.axis_index("fsdp")
@@ -59,15 +59,24 @@
         ahead, back = ((y + 1) % 4 * 2 + core) * wid, ((y + 3) % 4 * 2 + core) * wid
         return (
             ((((y + 2) % 4 * 2 + core) * wid, 0, wid),),
-            ((ahead, 0, 384), (back, 384, 256)),
-            ((ahead + 384, 0, 256), (back + 256, 256, 384)),
+            ((ahead, 0, 384), (back + 384, 384, 256)),
+            ((ahead + 384, 0, 256), (back, 256, 384)),
             (((y * 2 + core) * wid, 0, wid),),
         )[t2 // 2]
 
     def head_cols(d, hh):
         return pl.ds(pl.multiple_of(d * wid + hh * HD, 128), HD)
 
-    c_copy = pltpu.make_async_copy(c_hbm, c_ref, loc_sem.at[0])
+    c_copies = []
+    for t2 in range(8):
+        for k, (start, at, width) in enumerate(pieces(t2)):
+            c_copies.append(
+                pltpu.make_async_copy(
+                    c_hbm.at[:, :, pl.ds(pl.multiple_of(start, 128), width)],
+                    g_ref.at[t2, :, my_rows, pl.ds(at, width)],
+                    c_sem,
+                )
+            )
     gate_copy = pltpu.make_async_copy(gate_hbm, gate_ref, loc_sem.at[1])
     o_copy = pltpu.make_async_copy(o_hbm.at[:, :, col(h)], o_ref.at[:, my_rows, :], loc_sem.at[2])
     w_copies = []
@@ -75,7 +84,7 @@
         for k, (start, at, width) in enumerate(pieces(t2)):
             w_copies.append(
                 pltpu.make_async_copy(
-                    w_hbm.at[:, pl.ds(pl.multiple_of(start, 128), width)], w_ref.at[t2, :, pl.ds(at, width)], w_sem.at[t2, k]
+                    w_hbm.at[:, pl.ds(pl.multiple_of(start, 128), width)], w_ref.at[t2, :, pl.ds(at, width)], w_sem
                 )
             )
 
@@ -85,7 +94,7 @@
             (v_hbm, v_ref.at[hh, pl.ds(1, 2), my_rows, :]),
             (q_hbm, q_ref.at[hh, :, my_rows, :]),
         )[i]
-        return pltpu.make_async_copy(src.at[:, :, head_cols(h, hh)], dst, ex_recv.at[hh, i, 0])
+        return pltpu.make_async_copy(src.at[:, :, head_cols(h, hh)], dst, own_sem)
 
     barrier = pltpu.get_barrier_semaphore()
     for p in range(1, nh):
@@ -93,32 +102,18 @@
     for other in (right, left, up, down):
         pl.semaphore_signal(barrier, inc=1, device_id={"frame": other}, device_id_type=MESH)
     pl.semaphore_signal(barrier, inc=1, device_id={"fsdp": 1 - s}, device_id_type=MESH)
-    c_copy.start()
-    gate_copy.start()
-    o_copy.start()
-    for copy in w_copies:
+    for copy in c_copies:
         copy.start()
-
-    @pl.loop(0, heads)
-    def _(hh):
-        for i in range(3):
-            own_copy(i, hh).start()
-
-    c_copy.wait()
-    gate_copy.wait()
-    for t2 in range(8):
-        for start, at, width in pieces(t2):
-            cols = pl.ds(pl.multiple_of(start, 128), width)
-            for lf in range(2):
-                gain = gate_ref[pl.ds(levels[lf], 1), cols]
-                g_ref[t2, lf, my_rows, pl.ds(at, width)] = (c_ref[lf, :, cols].astype(jnp.float32) * gain).astype(jnp.bfloat16)
     pl.semaphore_wait(barrier, nh - 1 + 5)
+
+    def wait_bytes(ref, sem):
+        pltpu.make_async_copy(ref, ref, sem).wait()
 
     def o_exchange(p):
         d = (h + p) % nh
         return pltpu.make_async_remote_copy(
             src_ref=o_hbm.at[:, :, col(d)], dst_ref=o_ref.at[:, my_rows, :],
-            send_sem=exo_send.at[p], recv_sem=exo_recv.at[p],
+            send_sem=exo_send, recv_sem=exo_recv,
             device_id={"head": d}, device_id_type=MESH,
         )
 
@@ -131,14 +126,14 @@
         )[i]
         return pltpu.make_async_remote_copy(
             src_ref=src.at[:, :, head_cols(d, hh)], dst_ref=dst,
-            send_sem=ex_send.at[hh, i, p], recv_sem=ex_recv.at[hh, i, p],
+            send_sem=ex_send, recv_sem=ex_recv.at[hh, i // 2],
             device_id={"head": d}, device_id_type=MESH,
         )
 
     def part(t2, n, half, idx, xt, zt):
         ref = g_ref.at[t2, :, rows_of(n)] if half is None else g_ref.at[t2, half, rows_of(n)]
         return pltpu.make_async_remote_copy(
-            src_ref=ref, dst_ref=ref, send_sem=ag_send.at[t2, idx], recv_sem=ag_recv.at[t2, idx],
+            src_ref=ref, dst_ref=ref, send_sem=ag_send, recv_sem=ag_recv.at[t2, idx // 2] if idx < 4 else ag_part.at[t2],
             device_id={"head": xt * 4 + zt}, device_id_type=MESH,
         )
 
@@ -162,100 +157,114 @@
         gather(t2, 1).start()
 
     def stage2(t2):
-        gather(t2, 0).wait_recv()
-        gather(t2, 2).start()
-        gather(t2, 4).start()
-        gather(t2, 1).wait_recv()
-        gather(t2, 3).start()
-        gather(t2, 5).start()
+        wait_bytes(g_ref.at[t2, 0, pl.ds(0, 128)], ag_recv.at[t2, 0])
+        for idx in range(2, 6):
+            gather(t2, idx).start()
 
     def stage3(t2):
-        gather(t2, 2).wait_recv()
-        gather(t2, 6).start()
-        gather(t2, 7).start()
-        gather(t2, 3).wait_recv()
-        gather(t2, 8).start()
-        gather(t2, 9).start()
+        wait_bytes(g_ref.at[t2, 0, pl.ds(0, 128)], ag_recv.at[t2, 1])
+        for idx in range(6, 10):
+            gather(t2, idx).start()
 
     order = (4, 2, 6, 1, 7, 3, 5)
-    for t2 in range(4):
-        stage1(t2)
-    for p in order:
-        o_exchange(p).start()
 
     def halo(i, hh, which):
         ref = (k_ref, v_ref)[i]
         return pltpu.make_async_remote_copy(
             src_ref=ref.at[hh, 2 if which == 0 else 1], dst_ref=ref.at[hh, 0 if which == 0 else 3],
-            send_sem=halo_ssem.at[i, hh, which], recv_sem=halo_rsem.at[i, hh, which],
+            send_sem=halo_ssem, recv_sem=halo_rsem.at[hh],
             device_id={"frame": right if which == 0 else left}, device_id_type=MESH,
         )
 
     def s1(t):
         return pltpu.make_async_remote_copy(
-            src_ref=s1_send.at[t], dst_ref=s1_recv.at[t], send_sem=s1_ssem.at[t], recv_sem=s1_rsem.at[t],
+            src_ref=s1_send.at[t], dst_ref=s1_recv.at[t], send_sem=s1_ssem, recv_sem=s1_rsem.at[t],
             device_id={"frame": pair}, device_id_type=MESH,
         )
 
-    far_cols = (pl.ds(0, 384), pl.ds(384, 256))
-    near_cols = ((pl.ds(0, 384), pl.ds(384, 256)), (pl.ds(0, 256), pl.ds(256, 384)))
+    far_cols = (pl.ds(384, 256), pl.ds(0, 384))
+    near_cols = ((pl.ds(0, 384), pl.ds(384, 256)), (pl.ds(384, 256), pl.ds(0, 384)))
 
     def far(i):
         return pltpu.make_async_remote_copy(
             src_ref=far_send.at[:, far_cols[i]], dst_ref=far_recv.at[:, far_cols[i]],
-            send_sem=far_ssem.at[i], recv_sem=far_rsem.at[i],
+            send_sem=far_ssem, recv_sem=far_rsem.at[i],
             device_id={"frame": up if i == 0 else down}, device_id_type=MESH,
         )
 
     def near(i, r):
         return pltpu.make_async_remote_copy(
             src_ref=near_send.at[i, :, near_cols[i][r]], dst_ref=near_recv.at[i, :, near_cols[i][r]],
-            send_sem=near_ssem.at[i, r], recv_sem=near_rsem.at[i, r],
+            send_sem=near_ssem, recv_sem=near_rsem,
             device_id={"frame": up if i == 0 else down}, device_id_type=MESH,
         )
 
     def one_chunk(t2):
-        for idx in range(4, 10):
-            gather(t2, idx).wait_recv()
-        rhs = g_ref[t2].reshape(2 * TOKF, wid)
+        wait_bytes(g_ref.at[t2, 0, pl.ds(0, 192)], ag_part.at[t2])
+        gated = [
+            (g_ref[t2, lf].astype(jnp.float32) * gain_ref[t2, pl.ds(lf, 1), :]).astype(jnp.bfloat16) for lf in range(2)
+        ]
+        rhs = jnp.concatenate(gated, axis=0)
         dacc[...] += dot(rhs, w_ref[t2], NT)
         return dot(ot_ref[...], rhs, NN) * (1.0 / tokens_all)
 
     def send_near(i, r):
-        if (i, r) == (0, 0):
-            far(0).wait_recv()
-            near_send[0, :, pl.ds(0, 384)] = (gsum[1, :, pl.ds(0, 384)] + far_recv[:, pl.ds(0, 384)].astype(jnp.float32)).astype(
-                jnp.bfloat16
-            )
-        elif (i, r) == (1, 0):
-            near_send[1, :, pl.ds(0, 256)] = gsum[1, :, pl.ds(384, 256)].astype(jnp.bfloat16)
-        elif (i, r) == (0, 1):
-            near_send[0, :, pl.ds(384, 256)] = gsum[2, :, pl.ds(0, 256)].astype(jnp.bfloat16)
-        else:
-            far(1).wait_recv()
-            near_send[1, :, pl.ds(256, 128)] = gsum[2, :, pl.ds(256, 128)].astype(jnp.bfloat16)
-            near_send[1, :, pl.ds(384, 256)] = (gsum[2, :, pl.ds(384, 256)] + far_recv[:, pl.ds(384, 256)].astype(jnp.float32)).astype(
-                jnp.bfloat16
-            )
+        cols = near_cols[i][r]
+        held = ((pl.ds(0, 384), pl.ds(0, 256)), (pl.ds(384, 256), pl.ds(256, 384)))[i][r]
+        total = gsum[1 + r, :, held]
+        if r == 1:
+            far(i).wait_recv()
+            total = total + far_recv[:, cols].astype(jnp.float32)
+        near_send[i, :, cols] = total.astype(jnp.bfloat16)
         near(i, r).start()
 
-    def send_head(n):
-        @pl.when(n < heads)
-        def _():
-            for i in range(2):
-                for p in order:
-                    exchange(i, n, p).start()
-
-        @pl.when((n >= 1) & (n <= heads))
-        def _():
+    def send(names):
+        for i, n in names:
             for p in order:
-                exchange(2, n - 1, p).start()
-
-    def forward(tt, u):
-        @pl.when(tt < 4)
-        def _():
-            stage3(u)
-
+                exchange(i, n, p).start()
+
+    for t2 in range(2):
+        ((start, _, width),) = pieces(t2)
+        for idx, to in ((0, zp), (1, zm)):
+            pltpu.make_async_remote_copy(
+                src_ref=c_hbm.at[:, :, pl.ds(pl.multiple_of(start, 128), width)], dst_ref=g_ref.at[t2, :, my_rows],
+                send_sem=ag_send, recv_sem=ag_recv.at[t2, 0],
+                device_id={"head": xh * 4 + to}, device_id_type=MESH,
+            ).start()
+    for p in order[:3]:
+        o_exchange(p).start()
+    o_copy.start()
+    gate_copy.start()
+    for copy in w_copies:
+        copy.start()
+
+    @pl.loop(0, heads)
+    def _(hh):
+        for i in range(3):
+            own_copy(i, hh).start()
+
+    stage2(0)
+    pltpu.make_async_copy(g_ref.at[:, :, my_rows, :], g_ref.at[:, :, my_rows, :], c_sem).wait()
+    stage2(1)
+    for p in order[3:]:
+        o_exchange(p).start()
+    stage1(2)
+    stage1(3)
+    gate_copy.wait()
+    for t2 in range(8):
+        for start, at, width in pieces(t2):
+            for lf in range(2):
+                gain_ref[t2, pl.ds(lf, 1), pl.ds(at, width)] = gate_ref[
+                    pl.ds(levels[lf], 1), pl.ds(pl.multiple_of(start, 128), width)
+                ]
+
+    def take(n):
+        wait_bytes(k_ref.at[n, :, pl.ds(0, 224), :], ex_recv.at[n, 0])
+        for i in range(2):
+            halo(i, n, 0).start()
+            halo(i, n, 1).start()
+
+    def later(tt, u):
         @pl.when(tt < 3)
         def _():
             stage2(u + 2)
@@ -263,42 +272,16 @@
         @pl.when(tt < 2)
         def _():
             stage1(u + 4)
-
-    stage2(0)
-    stage2(1)
 
     @pl.loop(0, 5)
     def _(tt):
         t = tt - 1
 
-        forward(tt, 2 * tt)
-
-        @pl.when(tt == 0)
-        def _():
-            o_copy.wait()
-            for p in range(1, nh):
-                o_exchange(p).wait_recv()
-            for lf in range(2):
-                ot_ref[:, pl.ds(lf * TOKF, TOKF)] = o_ref[lf].astype(jnp.float32).T.astype(jnp.bfloat16)
-            for copy in w_copies:
-                copy.wait()
-            dacc[...] = jnp.zeros_like(dacc)
-
-        @pl.when(tt >= 1)
-        def _():
-            s1_send[t] = one_chunk(2 * t).astype(jnp.bfloat16)
-            s1(t).start()
-
-        forward(tt, 2 * tt + 1)
-
-        @pl.when(tt == 3)
-        def _():
-            for n in range(3):
-                send_head(n)
-
-        @pl.when(t == 2)
-        def _():
-            send_near(0, 0)
+        @pl.when(tt < 4)
+        def _():
+            stage3(2 * tt)
+
+        later(tt, 2 * tt)
 
         @pl.when(tt >= 1)
         def _():
@@ -314,12 +297,42 @@
 
         @pl.when(t == 1)
         def _():
+            send_near(0, 0)
             send_near(1, 0)
 
         @pl.when(t == 2)
         def _():
             send_near(0, 1)
             send_near(1, 1)
+
+        @pl.when(tt < 4)
+        def _():
+            stage3(2 * tt + 1)
+
+        later(tt, 2 * tt + 1)
+
+        @pl.when(tt == 3)
+        def _():
+            send(((0, 0), (1, 0), (2, 0), (0, 1), (1, 1)))
+
+        @pl.when(tt == 0)
+        def _():
+            o_copy.wait()
+            wait_bytes(o_ref.at[:, pl.ds(0, 224), :], exo_recv)
+            wait_bytes(o_ref.at[:, pl.ds(0, 224), :], exo_send)
+            for lf in range(2):
+                ot_ref[:, pl.ds(lf * TOKF, TOKF)] = o_ref[lf].astype(jnp.float32).T.astype(jnp.bfloat16)
+            wait_bytes(w_ref, w_sem)
+            wait_bytes(k_ref.at[0, :, pl.ds(0, 240), :], own_sem)
+            dacc[...] = jnp.zeros_like(dacc)
+
+        @pl.when(tt < 4)
+        def _():
+            s1_send[tt] = one_chunk(2 * tt).astype(jnp.bfloat16)
+            s1(tt).start()
+
+    send(((2, 1), (0, 2), (1, 2), (2, 2)))
+    take(0)
 
     x_copy = pltpu.make_async_remote_copy(
         src_ref=x_send, dst_ref=x_recv, send_sem=x_ssem, recv_sem=x_rsem,
@@ -327,9 +340,7 @@
     )
 
     def own_block():
-        for i in range(2):
-            for r in range(2):
-                near(i, r).wait_recv()
+        wait_bytes(near_recv, near_rsem)
         total = gsum[3] + near_recv[0].astype(jnp.float32) + near_recv[1].astype(jnp.float32)
         gsum[0] = total.T
         x_send[...] = gsum[0, pl.ds(pl.multiple_of(320 * (1 - s), 64), 320), :].astype(jnp.bfloat16)
@@ -337,7 +348,7 @@
 
     def halo_grad(i, hh):
         return pltpu.make_async_remote_copy(
-            src_ref=h_send.at[i, hh], dst_ref=h_recv.at[i, hh], send_sem=hg_ssem.at[i, hh], recv_sem=hg_rsem.at[i, hh],
+            src_ref=h_send.at[i, hh], dst_ref=h_recv.at[i, hh], send_sem=hg_ssem, recv_sem=hg_rsem.at[hh],
             device_id={"frame": left if i == 0 else right}, device_id_type=MESH,
         )
 
@@ -393,75 +404,49 @@
 
     def finish(hh):
         hs = pl.ds(pl.multiple_of(hh * HD, 128), HD)
-        halo_grad(0, hh).wait_recv()
-        halo_grad(1, hh).wait_recv()
+        wait_bytes(h_recv.at[:, hh], hg_rsem.at[hh])
         dk_ref[0, :, hs] = (own_k[hh, 0] + h_recv[1, hh, 0].astype(jnp.float32)).astype(jnp.bfloat16)
         dk_ref[1, :, hs] = (own_k[hh, 1] + h_recv[0, hh, 0].astype(jnp.float32)).astype(jnp.bfloat16)
         dv_ref[0, :, hs] = (own_v[hh, 0] + h_recv[1, hh, 1].astype(jnp.float32)).astype(jnp.bfloat16)
         dv_ref[1, :, hs] = (own_v[hh, 1] + h_recv[0, hh, 1].astype(jnp.float32)).astype(jnp.bfloat16)
 
-    @pl.loop(0, heads + 2)
+    wait_bytes(g_ref.at[:, :, pl.ds(0, 224), :], ag_send)
+    wait_bytes(s1_send, s1_ssem)
+    wait_bytes(far_send, far_ssem)
+    take(1)
+    send(((0, 3), (1, 3), (0, 4), (1, 4), (2, 3), (2, 4)))
+
+    @pl.loop(0, heads)
     def _(n):
-        @pl.when(n < heads)
-        def _():
-            for i in range(2):
-                own_copy(i, n).wait()
-                for p in range(1, nh):
-                    exchange(i, n, p).wait_recv()
-                halo(i, n, 0).start()
-                halo(i, n, 1).start()
-
-        @pl.when(n == 3)
+        @pl.when((n >= 1) & (n <= 2))
+        def _():
+            take(n + 1)
+
+        @pl.when(n == 1)
         def _():
             own_block()
 
-        send_head(n + 3)
-
-        @pl.when((n >= 1) & (n <= heads))
-        def _():
-            hh = n - 1
-            own_copy(2, hh).wait()
-            for p in range(1, nh):
-                exchange(2, hh, p).wait_recv()
-            for i in range(2):
-                halo(i, hh, 0).wait_recv()
-                halo(i, hh, 1).wait_recv()
-            attend(hh)
+        @pl.when(n == 2)
+        def _():
+            take(4)
+
+        wait_bytes(q_ref.at[n, :, pl.ds(0, 224), :], ex_recv.at[n, 1])
+        wait_bytes(k_ref.at[n], halo_rsem.at[n])
+        attend(n)
 
         @pl.when(n >= 2)
         def _():
             finish(n - 2)
 
+    finish(heads - 2)
+    wait_bytes(g_ref.at[pl.ds(0, 3), :, pl.ds(0, 224), :], ex_send)
+    wait_bytes(k_ref, halo_ssem)
+    wait_bytes(near_send, near_ssem)
+    x_copy.wait_send()
     x_copy.wait_recv()
     dw_ref[...] = gsum[0, pl.ds(pl.multiple_of(320 * s, 64), 320), :] + x_recv[...].astype(jnp.float32)
-
-    for p in range(1, nh):
-        o_exchange(p).wait_send()
-
-    @pl.loop(0, heads)
-    def _(hh):
-        for i in range(3):
-            for p in range(1, nh):
-                exchange(i, hh, p).wait_send()
-        for i in range(2):
-            halo(i, hh, 0).wait_send()
-            halo(i, hh, 1).wait_send()
-            halo_grad(i, hh).wait_send()
-
-    @pl.loop(0, 8)
-    def _(t2):
-        for idx in range(10):
-            gather(t2, idx).wait_send()
-
-    for i in range(2):
-        far(i).wait_send()
-        near(i, 0).wait_send()
-        near(i, 1).wait_send()
-    x_copy.wait_send()
-
-    @pl.loop(0, 4)
-    def _(t):
-        s1(t).wait_send()
+    finish(heads - 1)
+    wait_bytes(h_send, hg_ssem)
 
 
 def write_out(*refs):
@@ -495,8 +480,8 @@
             vm((2, TOKF, 640), bf),
             vm((5, 4, TOKF, HD), bf),
             vm((5, 4, TOKF, HD), bf),
-            vm((2, 32, 5120), bf),
             vm((LEVELS, 5120), f32),
+            vm((8, 2, 640), f32),
             vm((640, 2 * TOKF), bf),
             vm((2 * TOKF, 640), f32),
             vm((4, 640, 640), bf),
@@ -512,16 +497,16 @@
             vm((5, 2, TOKF, HD), f32),
             vm((2, 5, 2, TOKF, HD), bf),
             vm((2, 5, 2, TOKF, HD), bf),
-            dma((3,)), dma((8, 2)),
-            dma((8,)), dma((8,)),
-            dma((5, 3, 8)), dma((5, 3, 8)),
-            dma((8, 10)), dma((8, 10)),
-            dma((2, 5, 2)), dma((2, 5, 2)),
-            dma((4,)), dma((4,)),
-            dma((2,)), dma((2,)),
-            dma((2, 2)), dma((2, 2)),
+            dma((3,)), dma(()), dma(()), dma(()),
             dma(()), dma(()),
-            dma((2, 5)), dma((2, 5)),
+            dma(()), dma((5, 2)),
+            dma(()), dma((8, 2)), dma((8,)),
+            dma(()), dma((5,)),
+            dma(()), dma((4,)),
+            dma(()), dma((2,)),
+            dma(()), dma(()),
+            dma(()), dma(()),
+            dma(()), dma((5,)),
         ],
         compiler_params=pltpu.CompilerParams(
             collective_id=0, has_side_effects=True, vmem_limit_bytes=58 * 2**20

time: 92.8 us -> 88.7 us (0.956)
  Pallas kernels: 92 us -> 87.9 us
    pallas_call x1, Pallas kernels: 90.5 us -> 86.3 us  [per_device(): pl.pallas_call(functools.partial(kernel, tokens_all), out_shape=(out, out...]
where the time goes in v3:
time: 88.7 us; the launch traced here: 88.5 us
  Pallas kernels  87.9 us (99%)
    pallas_call x1, Pallas kernels, per_device(): pl.pallas_call(functools.partial(kernel, tokens_all), out_shape=(out, out...  86.3 us

profile of v3, /device:TPU:0, one launch (start us, length us, event | category | flops | bytes accessed | tf_op | source)
XLA Modules:
  0.0 88.5 jit_solution(11727873777987347919)
XLA Ops:
  0.6 86.3 %window_backward.1 = (bf16[2,256,640]{2,1,0:T(8,128)(2,1)S(1)}, bf16[2,256,640]{2,1,0:T(8,128)(2,1)S(1)}, bf16[2,256,640]{2,1,0:T(8,128)(2,1)S(1)}, f32[320,640]{1,0:T(8,128)S(1)}) custom-call(s32[2,16]{1,0:T(2,128)} %bitcast.15, s32[2]{0:T(128)} %levels.1, bf16[2,32,5120]{2,1,0:T(8,128)(2,1)} %bitcast.10, bf16[2,32,5120]{2,1,0:T(8,128)(2,1)} %bitcast.11, ...), custom_call_target="tpu_custom_call" | custom-call | tf_op jit(solution)/shard_map/window_backward/pallas_call | solution.py:471
  87.0 1.6 %write_out.1 = (bf16[2,256,640]{2,1,0:T(8,128)(2,1)}, bf16[2,256,640]{2,1,0:T(8,128)(2,1)}, bf16[2,256,640]{2,1,0:T(8,128)(2,1)}, f32[320,640]{1,0:T(8,128)}) custom-call(bf16[2,256,640]{2,1,0:T(8,128)(2,1)S(1)} %get-tuple-element.12.refs_0_, bf16[2,256,640]{2,1,0:T(8,128)(2,1)S(1)} %get-tuple-element.13.refs_1_, ...), custom_call_target="tpu_custom_call" | custom-call | tf_op jit(solution)/shard_map/write_out/pallas_call | solution.py:519

commit v4 on v3

--- a/solution.py
+++ b/solution.py
@@ -331,7 +331,7 @@
             s1_send[tt] = one_chunk(2 * tt).astype(jnp.bfloat16)
             s1(tt).start()
 
-    send(((2, 1), (0, 2), (1, 2), (2, 2)))
+    send(((0, 2), (1, 2), (2, 1), (0, 3), (1, 3), (0, 4), (1, 4), (2, 2), (2, 3), (2, 4)))
     take(0)
 
     x_copy = pltpu.make_async_remote_copy(
@@ -414,7 +414,6 @@
     wait_bytes(s1_send, s1_ssem)
     wait_bytes(far_send, far_ssem)
     take(1)
-    send(((0, 3), (1, 3), (0, 4), (1, 4), (2, 3), (2, 4)))
 
     @pl.loop(0, heads)
     def _(n):

time: 88.7 us -> 88.4 us (level)
  no operation moved by 1% of the time
where the time goes in v4:
time: 88.4 us; the launch traced here: 88.2 us
  Pallas kernels  87.6 us (99%)
    pallas_call x1, Pallas kernels, per_device(): pl.pallas_call(functools.partial(kernel, tokens_all), out_shape=(out, out...  86 us

profile of v4, /device:TPU:0, one launch (start us, length us, event | category | flops | bytes accessed | tf_op | source)
XLA Modules:
  0.0 88.2 jit_solution(12913712188113555922)
XLA Ops:
  0.6 86.0 %window_backward.1 = (bf16[2,256,640]{2,1,0:T(8,128)(2,1)S(1)}, bf16[2,256,640]{2,1,0:T(8,128)(2,1)S(1)}, bf16[2,256,640]{2,1,0:T(8,128)(2,1)S(1)}, f32[320,640]{1,0:T(8,128)S(1)}) custom-call(s32[2,16]{1,0:T(2,128)} %bitcast.15, s32[2]{0:T(128)} %levels.1, bf16[2,32,5120]{2,1,0:T(8,128)(2,1)} %bitcast.10, bf16[2,32,5120]{2,1,0:T(8,128)(2,1)} %bitcast.11, ...), custom_call_target="tpu_custom_call" | custom-call | tf_op jit(solution)/shard_map/window_backward/pallas_call | solution.py:470
  86.7 1.6 %write_out.1 = (bf16[2,256,640]{2,1,0:T(8,128)(2,1)}, bf16[2,256,640]{2,1,0:T(8,128)(2,1)}, bf16[2,256,640]{2,1,0:T(8,128)(2,1)}, f32[320,640]{1,0:T(8,128)}) custom-call(bf16[2,256,640]{2,1,0:T(8,128)(2,1)S(1)} %get-tuple-element.12.refs_0_, bf16[2,256,640]{2,1,0:T(8,128)(2,1)S(1)} %get-tuple-element.13.refs_1_, ...), custom_call_target="tpu_custom_call" | custom-call | tf_op jit(solution)/shard_map/write_out/pallas_call | solution.py:518

commit v5 on v4

--- a/solution.py
+++ b/solution.py
@@ -449,7 +449,11 @@
 
 
 def write_out(*refs):
-    copies = [pltpu.make_async_copy(refs[i], refs[4 + i], refs[8].at[i]) for i in range(4)]
+    copies = []
+    for i in range(4):
+        for half in range(2):
+            at = half if i < 3 else pl.ds(160 * half, 160)
+            copies.append(pltpu.make_async_copy(refs[i].at[at], refs[4 + i].at[at], refs[8].at[i, half]))
     for copy in copies:
         copy.start()
     for copy in copies:
@@ -520,7 +524,7 @@
         out_shape=(out, out, out, jax.ShapeDtypeStruct((320, 640), f32)),
         in_specs=[pl.BlockSpec(memory_space=vm)] * 4,
         out_specs=(hbm,) * 4,
-        scratch_shapes=[dma((4,))],
+        scratch_shapes=[dma((4, 2))],
         compiler_params=pltpu.CompilerParams(vmem_limit_bytes=4 * 2**20),
         name="write_out",
     )(*held)

time: 88.4 us -> 88.4 us (level)
  no operation moved by 1% of the time
where the time goes in v5:
time: 88.4 us; the launch traced here: 88.3 us
  Pallas kernels  87.6 us (99%)
    pallas_call x1, Pallas kernels, per_device(): pl.pallas_call(functools.partial(kernel, tokens_all), out_shape=(out, out...  86 us

profile of v5, /device:TPU:0, one launch (start us, length us, event | category | flops | bytes accessed | tf_op | source)
XLA Modules:
  0.0 88.3 jit_solution(14589271218033898709)
XLA Ops:
  0.6 86.0 %window_backward.1 = (bf16[2,256,640]{2,1,0:T(8,128)(2,1)S(1)}, bf16[2,256,640]{2,1,0:T(8,128)(2,1)S(1)}, bf16[2,256,640]{2,1,0:T(8,128)(2,1)S(1)}, f32[320,640]{1,0:T(8,128)S(1)}) custom-call(s32[2,16]{1,0:T(2,128)} %bitcast.15, s32[2]{0:T(128)} %levels.1, bf16[2,32,5120]{2,1,0:T(8,128)(2,1)} %bitcast.10, bf16[2,32,5120]{2,1,0:T(8,128)(2,1)} %bitcast.11, ...), custom_call_target="tpu_custom_call" | custom-call | tf_op jit(solution)/shard_map/window_backward/pallas_call | solution.py:474
  86.7 1.6 %write_out.1 = (bf16[2,256,640]{2,1,0:T(8,128)(2,1)}, bf16[2,256,640]{2,1,0:T(8,128)(2,1)}, bf16[2,256,640]{2,1,0:T(8,128)(2,1)}, f32[320,640]{1,0:T(8,128)}) custom-call(bf16[2,256,640]{2,1,0:T(8,128)(2,1)S(1)} %get-tuple-element.12.refs_0_, bf16[2,256,640]{2,1,0:T(8,128)(2,1)S(1)} %get-tuple-element.13.refs_1_, ...), custom_call_target="tpu_custom_call" | custom-call | tf_op jit(solution)/shard_map/write_out/pallas_call | solution.py:522
